TPU v7x, 32 devices: a whole 2x2x4 slice. The times are simulated.
32 devices in a mesh: tile: 8 (over z, y), obs: 4 (over x, core).
Axes of the slice: x: 2, y: 2, z: 4, core: 2. Of those that a mesh axis runs over, the one named last changes fastest.
Arguments:
- control: float32 [128, 512, 512], P(None, 'tile', 'obs'), may hold values from -6 to 6
- background: bfloat16 [128, 512, 512], P(None, 'tile', 'obs'), may hold values from -6 to 6
- spread: float32 [512, 512], P('tile', 'obs'), may hold values from 0.03 to 0.24
- obs_holder: int32 [8192, 1], P(('tile', 'obs')), may hold values from 0 to 31; in each aligned block of 256 rows (0 to 255, 256 to 511, ...) at most 24 rows name the same one
- obs_anchor: int32 [8192], P(('tile', 'obs')), may hold values from 0 to 8000
- obs_frac: float32 [2, 8192], P(None, ('tile', 'obs')), may hold values from 0 to 1
- innovation: float32 [8192, 616], P(('tile', 'obs')), may hold values from -6 to 6
- inverse_var: float32 [616], replicated, may hold values from 0.5 to 2
- w_first: bfloat16 [128, 512], replicated, may hold values from -0.5 to 0.5
- b_first: float32 [512], replicated, may hold values from -3 to 3
- w_second: bfloat16 [512, 512], replicated, may hold values from -0.25 to 0.25
- b_second: float32 [512], replicated, may hold values from -3 to 3
- w_third: bfloat16 [512, 616], replicated, may hold values from -0.25 to 0.25
Outputs:
- departures: float32 [8192, 616], P(('tile', 'obs'))
- gradient: float32 [128, 512, 512], P(None, 'tile', 'obs')
Inputs may be any that keep to these rules, and one draw needn't show every extreme that they name: `obs_holder`: among the observations of one device (aligned blocks of 256 rows) at most 24 name the same holder.
All inputs are finite; a program needn't handle non-finite values.
Results may differ from a plain program's by a relative error of at most 0.0011.
Values may be sent and summed in bfloat16 or wider, within the bound.
A program may use at most 64 MiB of HBM per device.

v0:
```python
import jax
import jax.numpy as jnp
from jax import lax
from jax.sharding import PartitionSpec as P

SWEEPS = 2


def padded_2(block, sides, width):
    for axis, dim in sides:
        count = lax.axis_size(axis)
        forward = [(i, i + 1) for i in range(count - 1)]
        forward.append((count - 1, 0))
        backward = [(target, source) for source, target in forward]
        low = lax.ppermute(
            lax.slice_in_dim(block, block.shape[dim] - width, None, axis=dim), axis, forward
        )
        high = lax.ppermute(lax.slice_in_dim(block, 0, width, axis=dim), axis, backward)
        block = jnp.concatenate([low, block, high], axis=dim)
    return block


def crop(array, cut):
    if cut == 0:
        return array
    return array[..., cut:-cut, cut:-cut]


def laplace(padded):
    total = padded[:, 2:, 1:-1] + padded[:, :-2, 1:-1]
    total = total + padded[:, 1:-1, 2:] + padded[:, 1:-1, :-2]
    return total - 4.0 * padded[:, 1:-1, 1:-1]


def advance(padded, margin, spread_pad, spread_margin, adjoint):
    if adjoint:
        scaled = crop(spread_pad, spread_margin - margin)[None] * padded
        return crop(padded, 1) + laplace(scaled)
    return crop(padded, 1) + crop(spread_pad, spread_margin - margin + 1)[None] * laplace(padded)


def diffuse(field, spread_pad, spread_margin, adjoint):
    padded = padded_2(field, (("tile", 1), ("obs", 2)), SWEEPS)
    for step in range(SWEEPS):
        padded = advance(padded, SWEEPS - step, spread_pad, spread_margin, adjoint)
    return padded


def corner_weights(frac_x, frac_y):
    return jnp.stack(
        [
            (1.0 - frac_x) * (1.0 - frac_y),
            frac_x * (1.0 - frac_y),
            (1.0 - frac_x) * frac_y,
            frac_x * frac_y,
        ],
        axis=1,
    )


def blend(columns, weights):
    return sum((weights[:, j, None] * columns[:, j].astype(jnp.float32) for j in range(4)))


def radiances(base, delta, innov, inverse_var, w_first, b_first, w_second, b_second, w_third):
    h_one = jnp.tanh(jnp.dot(base, w_first, preferred_element_type=jnp.float32) + b_first)
    d_one = 1.0 - h_one * h_one
    h_two = jnp.tanh(
        jnp.dot(h_one.astype(jnp.bfloat16), w_second, preferred_element_type=jnp.float32) + b_second
    )
    d_two = 1.0 - h_two * h_two
    t_one = (d_one * jnp.dot(delta, w_first, preferred_element_type=jnp.float32)).astype(
        jnp.bfloat16
    )
    t_two = (d_two * jnp.dot(t_one, w_second, preferred_element_type=jnp.float32)).astype(
        jnp.bfloat16
    )
    change = jnp.dot(t_two, w_third, preferred_element_type=jnp.float32)
    departures = (change - innov) * inverse_var
    s_two = (
        d_two
        * jnp.dot(departures.astype(jnp.bfloat16), w_third.T, preferred_element_type=jnp.float32)
    ).astype(jnp.bfloat16)
    s_one = (d_one * jnp.dot(s_two, w_second.T, preferred_element_type=jnp.float32)).astype(
        jnp.bfloat16
    )
    return (departures, jnp.dot(s_one, w_first.T, preferred_element_type=jnp.float32))


def per_device(
    control,
    background,
    spread,
    obs_holder,
    obs_anchor,
    obs_frac,
    innovation,
    inverse_var,
    w_first,
    b_first,
    w_second,
    b_second,
    w_third,
):
    levels, rows_x, rows_y = control.shape
    owners = lax.axis_size("tile") * lax.axis_size("obs")
    count = obs_anchor.shape[0]
    capacity = 3 * count // owners
    holder = obs_holder[:, 0]
    marks = (holder[:, None] == jnp.arange(owners, dtype=jnp.int32)[None, :]).astype(jnp.int32)
    before = jnp.cumsum(marks, axis=0) - marks
    position = holder * capacity + jnp.sum(before * marks, axis=1)
    asked = jnp.zeros((owners * capacity,), jnp.int32).at[position].set(obs_anchor)
    asked = lax.all_to_all(
        asked.reshape(owners, capacity), ("tile", "obs"), split_axis=0, concat_axis=0, tiled=True
    ).reshape(-1)
    corner = asked // (rows_y - 1) * rows_y + asked % (rows_y - 1)
    source = jnp.stack([corner, corner + rows_y, corner + 1, corner + rows_y + 1], axis=1)
    rim = SWEEPS
    spread_pad = padded_2(spread, (("tile", 0), ("obs", 1)), rim)
    increment = diffuse(control, spread_pad, rim, False)
    bg_cols = background.reshape(levels, rows_x * rows_y).T
    inc_cols = increment.astype(jnp.bfloat16).reshape(levels, rows_x * rows_y).T
    own_weights = corner_weights(obs_frac[0], obs_frac[1])
    bg_set, inc_set = (
        lax.all_to_all(
            bg_cols[source].reshape(owners, capacity, 4, levels),
            ("tile", "obs"),
            split_axis=0,
            concat_axis=0,
            tiled=True,
        ),
        lax.all_to_all(
            inc_cols[source].reshape(owners, capacity, 4, levels),
            ("tile", "obs"),
            split_axis=0,
            concat_axis=0,
            tiled=True,
        ),
    )
    base = blend(bg_set.reshape(-1, 4, levels)[position], own_weights).astype(jnp.bfloat16)
    delta = blend(inc_set.reshape(-1, 4, levels)[position], own_weights).astype(jnp.bfloat16)
    departures, profile_grad = radiances(
        base, delta, innovation, inverse_var, w_first, b_first, w_second, b_second, w_third
    )
    weighted = own_weights[:, :, None] * profile_grad[:, None, :]
    pieces = jnp.zeros((owners * capacity, 4, levels), jnp.float32).at[position].set(weighted)
    pieces = (
        lax.all_to_all(
            pieces.reshape(owners, capacity, 4, levels).astype(jnp.bfloat16),
            ("tile", "obs"),
            split_axis=0,
            concat_axis=0,
            tiled=True,
        )
        .astype(jnp.float32)
        .reshape(-1, 4, levels)
    )
    gathered = (
        jnp.zeros((rows_x * rows_y, levels), jnp.float32)
        .at[source.reshape(-1)]
        .add(pieces.reshape(-1, levels))
    )
    adjoint = gathered.T.reshape(levels, rows_x, rows_y)
    gradient = control + diffuse(adjoint, spread_pad, rim, True)
    return (departures, gradient)


def solution(mesh):
    return jax.shard_map(
        per_device,
        mesh=mesh,
        in_specs=(
            P(None, "tile", "obs"),
            P(None, "tile", "obs"),
            P("tile", "obs"),
            P(("tile", "obs"), None),
            P(("tile", "obs")),
            P(None, ("tile", "obs")),
            P(("tile", "obs"), None),
            P(),
            P(),
            P(),
            P(),
            P(),
            P(),
        ),
        out_specs=(P(("tile", "obs"), None), P(None, "tile", "obs")),
        check_vma=False,
    )
```

profile of v0, /device:TPU:0, one launch (start us, length us, event | category | flops | bytes accessed | tf_op | source)
XLA Modules:
  0.0 198.2 jit_solution(13530209489693220513)
XLA Ops:
  1.4 3.0 %collective-permute-start.4 = (f32[2,128]{1,0:T(2,128)S(1)}, f32[2,128]{1,0:T(2,128)S(1)}, u32[]{:S(2)}, u32[]{:S(2)}) collective-permute-start(f32[2,128]{1,0:T(2,128)S(1)} %get-tuple-element.30), channel_id=1, source_target_pairs={{0,4},{4,8},{8,12},{12,16},{16,20},{20,24},{24,28},{28,0},{1,5},{5... | collective-permute-start | bytes 3080 | tf_op jit(solution)/shard_map/ppermute | solution.py:15
  4.4 3.0 %collective-permute-start.5 = (f32[2,128]{1,0:T(2,128)S(1)}, f32[2,128]{1,0:T(2,128)S(1)}, u32[]{:S(2)}, u32[]{:S(2)}) collective-permute-start(f32[2,128]{1,0:T(2,128)S(1)} %get-tuple-element.31), channel_id=1, source_target_pairs={{4,0},{8,4},{12,8},{16,12},{20,16},{24,20},{28,24},{0,28},{5,1},{9... | collective-permute-start | bytes 3080 | tf_op jit(solution)/shard_map/ppermute | solution.py:18
  12.7 3.3 %all-to-all-start = ((s32[32,1,24]{2,1,0:T(1,128)}), s32[32,1,24]{2,1,0:T(1,128)S(1)}, u32[]{:S(2)}, u32[]{:S(2)}) async-start(s32[32,1,24]{2,1,0:T(1,128)} %bitcast.9), calls=%async_computation | async-start | bytes 32768 | tf_op jit(solution)/shard_map/all_to_all | solution.py:114
  16.0 5.4 %copy.56 = f32[128,64,128]{0,1,2:T(8,128)} copy(f32[128,64,128]{2,1,0:T(8,128)} %param.13) | data formatting | bytes 8388608 | tf_op args[0]
  30.7 3.3 %copy.49 = bf16[128,64,128]{0,2,1:T(8,128)(2,1)S(1)} copy(bf16[128,64,128]{2,1,0:T(8,128)(2,1)} %param.14) | data formatting | bytes 4194304 | tf_op args[1]
  36.8 11.5 %gather_fusion = bf16[3072,128]{1,0:T(8,128)(2,1)} fusion(bf16[8192,128]{1,0:T(8,128)(2,1)S(1)} %bitcast.127, s32[3072]{0:T(1024)S(1)} %broadcast_clamp_fusion), kind=kCustom, calls=%fused_computation | custom fusion | bytes 1585152 | tf_op jit(solution)/shard_map/gather | solution.py:127
  48.4 4.2 %all-to-all-start.1 = ((bf16[32,24,4,128]{3,2,1,0:T(4,128)(2,1)}), bf16[32,24,4,128]{3,2,1,0:T(4,128)(2,1)}, u32[]{:S(2)}, u32[]{:S(2)}) async-start(bf16[32,24,4,128]{3,2,1,0:T(4,128)(2,1)} %bitcast.14), calls=%async_computation.1 | async-start | bytes 1572864 | tf_op jit(solution)/shard_map/all_to_all | solution.py:126
  52.6 3.4 %pad_maximum_fusion = f32[128,68,132]{0,1,2:T(8,128)S(1)} fusion(f32[128,68,2]{0,1,2:T(8,128)S(1)} %collective-permute-done.3, f32[128,2,128]{0,1,2:T(2,128)S(1)} %collective-permute-done.1, f32[128,64,128]{0,1,2:T(8,128)} %copy.56, f32[128,2,128]{0,1,2:T(2,128)S(1)} %collective-permute-done, f32[128,68,2]{0,1,2:T(8,128)S(1)} %collective-permute-done.2), kind=kLoop, calls=%fused_computation.7 | loop fusion | flops 4595712 | bytes 9191424 | tf_op jit(solution)/shard_map/concatenate | solution.py:19
  56.0 5.2 %fusion.5 = f32[128,66,130]{0,1,2:T(8,128)S(1)} fusion(f32[128,68,2]{0,1,2:T(8,128)S(1)} %collective-permute-done.2, f32[128,2,128]{0,1,2:T(2,128)S(1)} %collective-permute-done.1, f32[128,64,128]{0,1,2:T(8,128)S(1)} %copy-done.2, f32[128,2,128]{0,1,2:T(2,128)S(1)} %collective-permute-done, f32[128,68,2]{0,1,2:T(8,128)S(1)} %collective-permute-done.3, ...), kind=kLoop, calls=%fused_computation.19 | loop fusion | flops 14277120 | bytes 22201872 | tf_op jit(solution)/shard_map/add | solution.py:39
  61.3 3.0 %fusion.13 = bf16[128,64,128]{0,1,2:T(8,128)(2,1)S(1)} fusion(f32[128,66,130]{0,1,2:T(8,128)S(1)} %fusion.5, f32[64,128]{0,1:T(8,128)S(1)} %copy-done.10), kind=kLoop, calls=%fused_computation.38 | loop fusion | flops 8388608 | bytes 23101440 | tf_op jit(solution)/shard_map/convert_element_type | solution.py:123
  65.7 11.5 %gather_fusion.2 = bf16[3072,128]{1,0:T(8,128)(2,1)} fusion(bf16[8192,128]{1,0:T(8,128)(2,1)S(1)} %bitcast.128, s32[3072]{0:T(1024)S(1)} %broadcast_clamp_fusion), kind=kCustom, calls=%fused_computation.2 | custom fusion | bytes 1585152 | tf_op jit(solution)/shard_map/gather | solution.py:134
  77.2 5.9 %all-to-all-start.2 = ((bf16[32,24,4,128]{3,2,1,0:T(4,128)(2,1)}), bf16[32,24,4,128]{3,2,1,0:T(4,128)(2,1)S(1)}, u32[]{:S(2)}, u32[]{:S(2)}) async-start(bf16[32,24,4,128]{3,2,1,0:T(4,128)(2,1)} %bitcast.130), calls=%async_computation.2 | async-start | bytes 1572864 | tf_op jit(solution)/shard_map/all_to_all | solution.py:133
  90.8 12.8 %all-to-all-done.2 = bf16[32,24,4,128]{3,2,1,0:T(4,128)(2,1)S(1)} async-done(((bf16[32,24,4,128]{3,2,1,0:T(4,128)(2,1)}), bf16[32,24,4,128]{3,2,1,0:T(4,128)(2,1)S(1)}, u32[]{:S(2)}, u32[]{:S(2)}) %all-to-all-start.2) | async-done | bytes 786464 | tf_op jit(solution)/shard_map/all_to_all | solution.py:133
  110.1 7.2 %scatter_fusion = f32[768,4,128]{2,1,0:T(4,128)S(1)} fusion(f32[768,4,128]{2,1,0:T(4,128)S(1)} %broadcast_in_dim.11, s32[256]{0:T(256)} %bitcast.140, f32[256,4,128]{2,1,0:T(4,128)S(1)} %broadcast_multiply_fusion.2), kind=kCustom, calls=%fused_computation.5 | custom fusion | bytes 1573888 | tf_op jit(solution)/shard_map/scatter | solution.py:147
  118.4 3.6 %all-to-all-start.3 = ((bf16[32,24,4,128]{3,2,1,0:T(4,128)(2,1)}), bf16[32,24,4,128]{3,2,1,0:T(4,128)(2,1)S(1)}, u32[]{:S(2)}, u32[]{:S(2)}) async-start(bf16[32,24,4,128]{3,2,1,0:T(4,128)(2,1)} %bitcast.31), calls=%async_computation.3 | async-start | bytes 1572864 | tf_op jit(solution)/shard_map/all_to_all | solution.py:149
  122.6 20.1 %all-to-all-done.3 = bf16[32,24,4,128]{3,2,1,0:T(4,128)(2,1)S(1)} async-done(((bf16[32,24,4,128]{3,2,1,0:T(4,128)(2,1)}), bf16[32,24,4,128]{3,2,1,0:T(4,128)(2,1)S(1)}, u32[]{:S(2)}, u32[]{:S(2)}) %all-to-all-start.3) | async-done | bytes 786464 | tf_op jit(solution)/shard_map/all_to_all | solution.py:149
  142.6 19.1 %scatter_custom_fusion.2 = f32[8192,128]{1,0:T(8,128)} fusion(s32[3072]{0:T(1024)S(1)} %bitcast.135, f32[]{:T(128)} %constant.49.clone.1, bf16[3072,128]{1,0:T(8,128)(2,1)S(1)} %bitcast.131), kind=kCustom, calls=%fused_computation.43 | custom fusion | flops 786432 | bytes 4980740 | tf_op jit(solution)/shard_map/scatter-add | solution.py:162
  161.8 4.6 %copy.68 = f32[128,64,128]{0,1,2:T(8,128)S(1)} copy(f32[128,64,128]{0,2,1:T(8,128)} %bitcast.129) | data formatting | bytes 8388608 | tf_op jit(solution)/shard_map/reshape | solution.py:164
  168.1 3.2 %collective-permute-start.9 = (f32[128,2,128]{0,1,2:T(2,128)S(1)}, f32[128,2,128]{0,1,2:T(2,128)S(1)}, u32[]{:S(2)}, u32[]{:S(2)}) collective-permute-start(f32[128,2,128]{0,1,2:T(2,128)S(1)} %get-tuple-element.17), channel_id=1, source_target_pairs={{4,0},{8,4},{12,8},{16,12},{20,16},{24,20},{28,24},{0,28},{5,1},{9... | collective-permute-start | bytes 393224 | tf_op jit(solution)/shard_map/ppermute | solution.py:18
  171.3 3.4 %collective-permute-done.8 = f32[128,2,128]{0,1,2:T(2,128)S(1)} collective-permute-done((f32[128,2,128]{0,1,2:T(2,128)S(1)}, f32[128,2,128]{0,1,2:T(2,128)S(1)}, u32[]{:S(2)}, u32[]{:S(2)}) %collective-permute-start.8) | collective-permute-done | bytes 131104 | tf_op jit(solution)/shard_map/ppermute | solution.py:15
  179.7 4.7 %pad_maximum_fusion.1 = (f32[128,68,132]{0,1,2:T(8,128)S(1)}, f32[128,68,132]{0,1,2:T(8,128)S(1)}) fusion(f32[128,68,2]{0,1,2:T(8,128)S(1)} %collective-permute-done.11, f32[128,2,128]{0,1,2:T(2,128)S(1)} %collective-permute-done.9, f32[128,64,128]{0,1,2:T(8,128)} %copy-done.4, f32[128,2,128]{0,1,2:T(2,128)S(1)} %collective-permute-done.8, ...), kind=kLoop, calls=%fused_computation.8 | loop fusion | flops 5744640 | bytes 13823040 | tf_op jit(solution)/shard_map/concatenate | solution.py:19
  184.4 3.9 %broadcast_multiply_fusion.1 = (f32[128,66,130]{0,1,2:T(8,128)S(1)}, f32[128,66,130]{0,1,2:T(8,128)S(1)}) fusion(f32[66,130]{0,1:T(8,128)S(1)} %copy.59, f32[128,68,132]{0,1,2:T(8,128)S(1)} %get-tuple-element.11, f32[128,68,132]{0,1,2:T(8,128)S(1)} %get-tuple-element.10), kind=kLoop, calls=%fused_computation.42 | loop fusion | flops 7687680 | bytes 35178000 | tf_op jit(solution)/shard_map/mul | solution.py:37
  188.3 4.5 %fusion.9 = f32[128,64,128]{0,1,2:T(8,128)} fusion(f32[128,64,128]{0,1,2:T(8,128)S(1)} %copy-done.3, f32[128,66,130]{0,1,2:T(8,128)S(1)} %get-tuple-element.6, f32[128,66,130]{0,1,2:T(8,128)S(1)} %get-tuple-element.7), kind=kLoop, calls=%fused_computation.30 | loop fusion | flops 7340032 | bytes 33554432 | tf_op jit(solution)/shard_map/add | solution.py:165
  192.8 5.4 %copy.73 = f32[128,64,128]{2,1,0:T(8,128)} copy(f32[128,64,128]{0,1,2:T(8,128)} %fusion.9) | data formatting | bytes 8388608
  (106 shorter events, 41.7 us)
Async XLA Ops:
  0.6 106.5 %copy-start = (bf16[512,616]{0,1:T(8,128)(2,1)S(1)}, bf16[512,616]{0,1:T(8,128)(2,1)}, u32[]{:S(2)}) copy-start(bf16[512,616]{0,1:T(8,128)(2,1)} %param.25) | copy-start | bytes 1892356
  0.6 20.8 %copy-start.9 = (f32[64,128]{1,0:T(8,128)S(1)}, f32[64,128]{1,0:T(8,128)}, u32[]{:S(2)}) copy-start(f32[64,128]{1,0:T(8,128)} %param.15) | copy-start | bytes 98308
  1.4 20.0 %collective-permute-start.4 = (f32[2,128]{1,0:T(2,128)S(1)}, f32[2,128]{1,0:T(2,128)S(1)}, u32[]{:S(2)}, u32[]{:S(2)}) collective-permute-start(f32[2,128]{1,0:T(2,128)S(1)} %get-tuple-element.30), channel_id=1, source_target_pairs={{0,4},{4,8},{8,12},{12,16},{16,20},{20,24},{24,28},{28,0},{1,5},{5... | collective-permute-start | bytes 3080 | tf_op jit(solution)/shard_map/ppermute | solution.py:15
  4.4 17.0 %collective-permute-start.5 = (f32[2,128]{1,0:T(2,128)S(1)}, f32[2,128]{1,0:T(2,128)S(1)}, u32[]{:S(2)}, u32[]{:S(2)}) collective-permute-start(f32[2,128]{1,0:T(2,128)S(1)} %get-tuple-element.31), channel_id=1, source_target_pairs={{4,0},{8,4},{12,8},{16,12},{20,16},{24,20},{28,24},{0,28},{5,1},{9... | collective-permute-start | bytes 3080 | tf_op jit(solution)/shard_map/ppermute | solution.py:18
  10.4 19.6 %copy-start.13 = (s32[256,1]{0,1:T(1,128)}, s32[256,1]{0,1:T(1,128)S(1)}, u32[]{:S(2)}) copy-start(s32[256,1]{0,1:T(1,128)S(1)} %compare_select_fusion.2) | copy-start | bytes 3076
  12.7 21.7 %all-to-all-start = ((s32[32,1,24]{2,1,0:T(1,128)}), s32[32,1,24]{2,1,0:T(1,128)S(1)}, u32[]{:S(2)}, u32[]{:S(2)}) async-start(s32[32,1,24]{2,1,0:T(1,128)} %bitcast.9), calls=%async_computation | async-start | bytes 32768 | tf_op jit(solution)/shard_map/all_to_all | solution.py:114
  21.5 12.5 %collective-permute-start.6 = (f32[68,2]{1,0:T(8,128)S(1)}, f32[68,2]{1,0:T(8,128)S(1)}, u32[]{:S(2)}, u32[]{:S(2)}) collective-permute-start(f32[68,2]{1,0:T(8,128)S(1)} %get-tuple-element.28), channel_id=1, source_target_pairs={{0,1},{1,2},{2,3},{3,0},{4,5},{5,6},{6,7},{7,4},{8,9},{9,10},{10,1... | collective-permute-start | bytes 1640 | tf_op jit(solution)/shard_map/ppermute | solution.py:15
  21.8 12.3 %collective-permute-start.7 = (f32[68,2]{1,0:T(8,128)S(1)}, f32[68,2]{1,0:T(8,128)S(1)}, u32[]{:S(2)}, u32[]{:S(2)}) collective-permute-start(f32[68,2]{1,0:T(8,128)S(1)} %get-tuple-element.29), channel_id=1, source_target_pairs={{1,0},{2,1},{3,2},{0,3},{5,4},{6,5},{7,6},{4,7},{9,8},{10,9},{11,1... | collective-permute-start | bytes 1640 | tf_op jit(solution)/shard_map/ppermute | solution.py:18
  25.3 10.1 %collective-permute-start = (f32[128,2,128]{0,1,2:T(2,128)}, f32[128,2,128]{0,1,2:T(2,128)S(1)}, u32[]{:S(2)}, u32[]{:S(2)}) collective-permute-start(f32[128,2,128]{0,1,2:T(2,128)} %get-tuple-element.18), channel_id=1, source_target_pairs={{0,4},{4,8},{8,12},{12,16},{16,20},{20,24},{24,28},{28,0},{1,5},{5... | collective-permute-start | bytes 393224 | tf_op jit(solution)/shard_map/ppermute | solution.py:15
  27.0 8.3 %collective-permute-start.1 = (f32[128,2,128]{0,1,2:T(2,128)}, f32[128,2,128]{0,1,2:T(2,128)S(1)}, u32[]{:S(2)}, u32[]{:S(2)}) collective-permute-start(f32[128,2,128]{0,1,2:T(2,128)} %get-tuple-element.19), channel_id=1, source_target_pairs={{4,0},{8,4},{12,8},{16,12},{20,16},{24,20},{28,24},{0,28},{5,1},{9... | collective-permute-start | bytes 393224 | tf_op jit(solution)/shard_map/ppermute | solution.py:18
  36.3 16.3 %collective-permute-start.3 = (f32[128,68,2]{0,1,2:T(8,128)S(1)}, f32[128,68,2]{0,1,2:T(8,128)S(1)}, u32[]{:S(2)}, u32[]{:S(2)}) collective-permute-start(f32[128,68,2]{0,1,2:T(8,128)S(1)} %get-tuple-element.14), channel_id=1, source_target_pairs={{1,0},{2,1},{3,2},{0,3},{5,4},{6,5},{7,6},{4,7},{9,8},{10,9},{11,1... | collective-permute-start | bytes 208904 | tf_op jit(solution)/shard_map/ppermute | solution.py:18
  36.3 16.2 %collective-permute-start.2 = (f32[128,68,2]{0,1,2:T(8,128)S(1)}, f32[128,68,2]{0,1,2:T(8,128)S(1)}, u32[]{:S(2)}, u32[]{:S(2)}) collective-permute-start(f32[128,68,2]{0,1,2:T(8,128)S(1)} %get-tuple-element.15), channel_id=1, source_target_pairs={{0,1},{1,2},{2,3},{3,0},{4,5},{5,6},{6,7},{7,4},{8,9},{9,10},{10,1... | collective-permute-start | bytes 208904 | tf_op jit(solution)/shard_map/ppermute | solution.py:15
  48.4 28.9 %all-to-all-start.1 = ((bf16[32,24,4,128]{3,2,1,0:T(4,128)(2,1)}), bf16[32,24,4,128]{3,2,1,0:T(4,128)(2,1)}, u32[]{:S(2)}, u32[]{:S(2)}) async-start(bf16[32,24,4,128]{3,2,1,0:T(4,128)(2,1)} %bitcast.14), calls=%async_computation.1 | async-start | bytes 1572864 | tf_op jit(solution)/shard_map/all_to_all | solution.py:126
  65.7 23.1 %copy-start.7 = (bf16[128,512]{1,0:T(8,128)(2,1)S(1)}, bf16[128,512]{1,0:T(8,128)(2,1)}, u32[]{:S(2)}) copy-start(bf16[128,512]{1,0:T(8,128)(2,1)} %param.21) | copy-start | bytes 393220
  65.7 24.1 %copy-start.5 = (bf16[512,512]{1,0:T(8,128)(2,1)S(1)}, bf16[512,512]{1,0:T(8,128)(2,1)}, u32[]{:S(2)}) copy-start(bf16[512,512]{1,0:T(8,128)(2,1)} %param.23) | copy-start | bytes 1572868
  77.2 26.4 %all-to-all-start.2 = ((bf16[32,24,4,128]{3,2,1,0:T(4,128)(2,1)}), bf16[32,24,4,128]{3,2,1,0:T(4,128)(2,1)S(1)}, u32[]{:S(2)}, u32[]{:S(2)}) async-start(bf16[32,24,4,128]{3,2,1,0:T(4,128)(2,1)} %bitcast.130), calls=%async_computation.2 | async-start | bytes 1572864 | tf_op jit(solution)/shard_map/all_to_all | solution.py:133
  86.2 17.4 %copy-start.11 = (f32[256]{0:T(256)}, f32[256]{0:T(256)S(1)}, u32[]{:S(2)}) copy-start(f32[256]{0:T(256)S(1)} %get-tuple-element.43) | copy-start | bytes 3076
  86.2 17.4 %copy-start.12 = (f32[256]{0:T(256)}, f32[256]{0:T(256)S(1)}, u32[]{:S(2)}) copy-start(f32[256]{0:T(256)S(1)} %get-tuple-element.44) | copy-start | bytes 3076
  118.4 24.2 %all-to-all-start.3 = ((bf16[32,24,4,128]{3,2,1,0:T(4,128)(2,1)}), bf16[32,24,4,128]{3,2,1,0:T(4,128)(2,1)S(1)}, u32[]{:S(2)}, u32[]{:S(2)}) async-start(bf16[32,24,4,128]{3,2,1,0:T(4,128)(2,1)} %bitcast.31), calls=%async_computation.3 | async-start | bytes 1572864 | tf_op jit(solution)/shard_map/all_to_all | solution.py:149
  166.5 8.1 %collective-permute-start.8 = (f32[128,2,128]{0,1,2:T(2,128)S(1)}, f32[128,2,128]{0,1,2:T(2,128)S(1)}, u32[]{:S(2)}, u32[]{:S(2)}) collective-permute-start(f32[128,2,128]{0,1,2:T(2,128)S(1)} %get-tuple-element.16), channel_id=1, source_target_pairs={{0,4},{4,8},{8,12},{12,16},{16,20},{20,24},{24,28},{28,0},{1,5},{5... | collective-permute-start | bytes 393224 | tf_op jit(solution)/shard_map/ppermute | solution.py:15
  168.1 7.8 %collective-permute-start.9 = (f32[128,2,128]{0,1,2:T(2,128)S(1)}, f32[128,2,128]{0,1,2:T(2,128)S(1)}, u32[]{:S(2)}, u32[]{:S(2)}) collective-permute-start(f32[128,2,128]{0,1,2:T(2,128)S(1)} %get-tuple-element.17), channel_id=1, source_target_pairs={{4,0},{8,4},{12,8},{16,12},{20,16},{24,20},{28,24},{0,28},{5,1},{9... | collective-permute-start | bytes 393224 | tf_op jit(solution)/shard_map/ppermute | solution.py:18
  175.9 3.8 %collective-permute-start.10 = (f32[128,68,2]{0,1,2:T(8,128)S(1)}, f32[128,68,2]{0,1,2:T(8,128)S(1)}, u32[]{:S(2)}, u32[]{:S(2)}) collective-permute-start(f32[128,68,2]{0,1,2:T(8,128)S(1)} %get-tuple-element.12), channel_id=1, source_target_pairs={{0,1},{1,2},{2,3},{3,0},{4,5},{5,6},{6,7},{7,4},{8,9},{9,10},{10,1... | collective-permute-start | bytes 208904 | tf_op jit(solution)/shard_map/ppermute | solution.py:15
  175.9 3.8 %collective-permute-start.11 = (f32[128,68,2]{0,1,2:T(8,128)S(1)}, f32[128,68,2]{0,1,2:T(8,128)S(1)}, u32[]{:S(2)}, u32[]{:S(2)}) collective-permute-start(f32[128,68,2]{0,1,2:T(8,128)S(1)} %get-tuple-element.13), channel_id=1, source_target_pairs={{1,0},{2,1},{3,2},{0,3},{5,4},{6,5},{7,6},{4,7},{9,8},{10,9},{11,1... | collective-permute-start | bytes 208904 | tf_op jit(solution)/shard_map/ppermute | solution.py:18
  188.3 9.9 %copy-start.1 = (bf16[512,616]{0,1:T(8,128)(2,1)S(1)}, bf16[512,616]{0,1:T(8,128)(2,1)}, u32[]{:S(2)}) copy-start(bf16[512,616]{0,1:T(8,128)(2,1)} %param.25) | copy-start | bytes 1892356
  (6 other events, 27.9 us)
where the time goes:
time: 200 us; the launch traced here: 198 us
  local copies, waits for them, and re-layouts  63.9 us (32%)
  other arithmetic  51.3 us (26%)
  waiting for transfers between devices  39.4 us (20%)
  starting transfers between devices  36.7 us (18%)
  matrix products  5.8 us (3%)
    all_to_all x1, waiting for transfers between devices, per_device(): lax.all_to_all(pieces.reshape(owners, capacity, 4, levels).astype(jnp.bfl...  20.1 us
    scatter-add x1, other arithmetic, per_device(): gathered = jnp.zeros((rows_x * rows_y, levels), jnp.float32).at[source.re...  19.1 us
    unnamed x32, local copies, waits for them, and re-layouts  14.9 us
    all_to_all x1, waiting for transfers between devices, per_device(): lax.all_to_all(inc_cols[source].reshape(owners, capacity, 4, levels), ('t...  12.8 us
    ppermute x6, starting transfers between devices, padded_2(): lax.ppermute(lax.slice_in_dim(block, 0, width, axis=dim), axis, backward)  12.5 us
    gather x1, local copies, waits for them, and re-layouts, per_device(): inc_cols[source].reshape(owners, capacity, 4, levels)  11.5 us
    gather x1, local copies, waits for them, and re-layouts, per_device(): bg_cols[source].reshape(owners, capacity, 4, levels)  11.5 us
    concatenate x5, other arithmetic, padded_2(): block = jnp.concatenate([low, block, high], axis=dim)  9.07 us
  transfers between devices with their start and end apart: 16, of which 5 were waited for; matrix products, arithmetic and copies ran while one was open for 31% of the time, Pallas kernels for 0%

commit v1 on v0

v1 whole, which is shorter than its diff:
```python
import functools

import jax
import jax.numpy as jnp
from jax import lax
from jax.experimental import pallas as pl
from jax.experimental.pallas import tpu as pltpu
from jax.sharding import PartitionSpec as P

SWEEPS = 2
LANES = 128
MESH_ID = pl.DeviceIdType.MESH
F32 = jnp.float32
BF16 = jnp.bfloat16


def vmem(count):
    return [pl.BlockSpec(memory_space=pltpu.VMEM)] * count


def split_two(value):
    high = value.astype(BF16)
    return high, (value - high.astype(F32)).astype(BF16)


def request_kernel(cap, per_row, holder_ref, anchor_ref, frac_ref, req_ref, pos_ref):
    owners = req_ref.shape[0]
    count = holder_ref.shape[0]
    holder = holder_ref[...]
    marks = holder == lax.broadcasted_iota(jnp.int32, (count, owners), 1)
    marks = marks.astype(F32)
    tri = lax.broadcasted_iota(jnp.int32, (count, count), 0) > lax.broadcasted_iota(
        jnp.int32, (count, count), 1
    )
    before = jnp.dot(
        tri.astype(F32).astype(BF16), marks.astype(BF16), preferred_element_type=F32
    )
    rank = jnp.sum(before * marks, axis=1, keepdims=True).astype(jnp.int32)
    pos_ref[...] = holder * cap + rank
    slot = holder * LANES + rank
    anchor = anchor_ref[...].astype(F32)
    ax = jnp.floor((anchor + 0.5) / per_row)
    ay = anchor - ax * per_row
    rows = [ax, ay]
    for axis in range(2):
        value = frac_ref[pl.ds(axis, 1), :]
        for _ in range(3):
            part = value.astype(BF16).astype(F32)
            rows.append(part)
            value = value - part
    index = lax.broadcasted_iota(jnp.int32, (8, count), 0)
    fields = jnp.zeros((8, count), F32)
    for k, row in enumerate(rows):
        fields = jnp.where(index == k, jnp.broadcast_to(row, (8, count)), fields)
    fields = fields.astype(BF16)
    step = 8
    for first in range(0, owners, step):
        lane = lax.broadcasted_iota(jnp.int32, (count, step * LANES), 1) + first * LANES
        chosen = (slot == lane).astype(F32).astype(BF16)
        got = jnp.dot(fields, chosen, preferred_element_type=F32)
        for k in range(step):
            req_ref[first + k] = got[:, k * LANES : (k + 1) * LANES]


def halo_copies(n_tile, n_obs, k, refs, send_sem, recv_sem):
    rows_ref, strips_ref, rows_out, strips_out, corners_out = refs
    tile, obs = lax.axis_index("tile"), lax.axis_index("obs")
    up, down = lax.rem(tile + n_tile - 1, n_tile), lax.rem(tile + 1, n_tile)
    west, east = lax.rem(obs + n_obs - 1, n_obs), lax.rem(obs + 1, n_obs)
    length = strips_ref.shape[1]
    top, end = pl.ds(0, 8), pl.ds(length - 8, 8)
    west_set, east_set = pl.ds(0, 2 * k), pl.ds(2 * k, 2 * k)
    west_edge, east_edge = pl.ds(0, k), pl.ds(2 * k, k)
    plan = [
        (rows_ref.at[pl.ds(0, 2)], rows_out.at[pl.ds(0, 2)], (up, obs)),
        (rows_ref.at[pl.ds(2, 2)], rows_out.at[pl.ds(2, 2)], (down, obs)),
        (strips_ref.at[west_set], strips_out.at[west_set], (tile, west)),
        (strips_ref.at[east_set], strips_out.at[east_set], (tile, east)),
        (strips_ref.at[west_edge, top], corners_out.at[0], (up, west)),
        (strips_ref.at[west_edge, end], corners_out.at[1], (down, west)),
        (strips_ref.at[east_edge, top], corners_out.at[2], (up, east)),
        (strips_ref.at[east_edge, end], corners_out.at[3], (down, east)),
    ]
    peers = [target for _, _, target in plan]
    copies = [
        pltpu.make_async_remote_copy(
            src_ref=source,
            dst_ref=target,
            send_sem=send_sem.at[i],
            recv_sem=recv_sem.at[i],
            device_id=peer,
            device_id_type=MESH_ID,
        )
        for i, (source, target, peer) in enumerate(plan)
    ]
    return peers, copies


def halo_kernel(n_tile, n_obs, k, rows_ref, strips_ref, rows_out, strips_out, corners_out, send_sem, recv_sem):
    peers, copies = halo_copies(
        n_tile, n_obs, k, (rows_ref, strips_ref, rows_out, strips_out, corners_out), send_sem, recv_sem
    )
    barrier = pltpu.get_barrier_semaphore()
    for peer in peers:
        pl.semaphore_signal(barrier, inc=1, device_id=peer, device_id_type=MESH_ID)
    pl.semaphore_wait(barrier, len(peers))
    for copy in copies:
        copy.start()
    for copy in copies:
        copy.wait()


def halo(rows, strips, n_tile, n_obs, k, ident):
    length = strips.shape[2]
    return pl.pallas_call(
        functools.partial(halo_kernel, n_tile, n_obs, k),
        out_shape=(
            jax.ShapeDtypeStruct(rows.shape, rows.dtype),
            jax.ShapeDtypeStruct(strips.shape, strips.dtype),
            jax.ShapeDtypeStruct((4, k, 8, length), strips.dtype),
        ),
        in_specs=vmem(2),
        out_specs=vmem(3),
        scratch_shapes=[pltpu.SemaphoreType.DMA((8,)), pltpu.SemaphoreType.DMA((8,))],
        compiler_params=pltpu.CompilerParams(collective_id=ident, has_side_effects=True),
        name="halo",
    )(rows, strips)


def swap_kernel(n_tile, n_obs, x_ref, out_ref, send_sem, recv_sem, own_sem):
    n = n_tile * n_obs
    me = lax.axis_index("tile") * n_obs + lax.axis_index("obs")

    def spot(k):
        peer = lax.rem(me + k, n)
        return peer, (peer // n_obs, lax.rem(peer, n_obs))

    barrier = pltpu.get_barrier_semaphore()

    def greet(k, _):
        pl.semaphore_signal(barrier, inc=1, device_id=spot(k)[1], device_id_type=MESH_ID)
        return 0

    lax.fori_loop(1, n, greet, 0)
    own = pltpu.make_async_copy(x_ref.at[me], out_ref.at[me], own_sem)
    own.start()
    pl.semaphore_wait(barrier, n - 1)

    def transfer(k):
        peer, place = spot(k)
        return pltpu.make_async_remote_copy(
            src_ref=x_ref.at[peer],
            dst_ref=out_ref.at[me],
            send_sem=send_sem.at[k],
            recv_sem=recv_sem.at[k],
            device_id=place,
            device_id_type=MESH_ID,
        )

    def begin(k, _):
        transfer(k).start()
        return 0

    def finish(k, _):
        transfer(k).wait()
        return 0

    lax.fori_loop(1, n, begin, 0)
    lax.fori_loop(1, n, finish, 0)
    own.wait()


def swap(x, n_tile, n_obs, ident):
    n = n_tile * n_obs
    return pl.pallas_call(
        functools.partial(swap_kernel, n_tile, n_obs),
        out_shape=jax.ShapeDtypeStruct(x.shape, x.dtype),
        in_specs=vmem(1),
        out_specs=pl.BlockSpec(memory_space=pltpu.VMEM),
        scratch_shapes=[
            pltpu.SemaphoreType.DMA((n,)),
            pltpu.SemaphoreType.DMA((n,)),
            pltpu.SemaphoreType.DMA,
        ],
        compiler_params=pltpu.CompilerParams(collective_id=ident, has_side_effects=True),
        name="swap",
    )(x)


def weight_fields(req, rows_x, rows_y):
    slots = req.shape[1]
    ax, ay = req[0:1].astype(jnp.int32), req[1:2].astype(jnp.int32)
    fx = req[2:3] + req[3:4] + req[4:5]
    fy = req[5:6] + req[6:7] + req[7:8]

    def ramp(size, place, frac):
        index = lax.broadcasted_iota(jnp.int32, (size, slots), 0)
        return jnp.where(index == place, 1.0 - frac, jnp.where(index == place + 1, frac, 0.0))

    return ramp(rows_x, ax, fx), ramp(rows_y, ay, fy)


def compact_kernel(cap, req_ref, out_ref):
    owners = req_ref.shape[0]
    out_ref[...] = jnp.concatenate([req_ref[p][:, :cap] for p in range(owners)], axis=1)


def around(value, axis):
    size = value.shape[axis]
    return pltpu.roll(value, 1, axis) + pltpu.roll(value, size - 1, axis)


def strip_setup(k, adjoint, own_ref, strips_ref, corners_ref, dstrips, edge_ref):
    length, levels = own_ref.shape[1], own_ref.shape[2]
    index = lax.broadcasted_iota(jnp.int32, (8, levels), 0)
    strips_d, corners_d, own_d = dstrips

    def extended(base, low, high):
        return jnp.concatenate([base, jnp.where(index < 4, low, high)], axis=0)

    def plain(base):
        return jnp.concatenate([base, jnp.zeros((8, levels), F32)], axis=0)

    for side, (near, far, own, corner_low, corner_high) in enumerate(
        ((2, 3, 0, 2, 3), (0, 1, 1, 0, 1))
    ):
        s_near = extended(strips_ref[near * k], corners_ref[corner_low, 0], corners_ref[corner_high, 0])
        s_far, s_own = plain(strips_ref[far * k]), plain(own_ref[own])
        d_near = extended(strips_d[near * 2 + 1], corners_d[corner_low, 1], corners_d[corner_high, 1])
        if adjoint:
            d_far, d_own = plain(strips_d[far * 2 + 1]), plain(own_d[own])
            h_near = d_near * s_near
            first = s_near + around(h_near, 0) + d_far * s_far + d_own * s_own - 4.0 * h_near
            edge_ref[side] = h_near
            edge_ref[2 + side] = d_near * first
        else:
            first = s_near + d_near * (around(s_near, 0) + s_far + s_own - 4.0 * s_near)
            edge_ref[side] = s_near
            edge_ref[2 + side] = first


def extend_rows(block, rows_ref, level):
    index = lax.broadcasted_iota(jnp.int32, (8, block.shape[1]), 0)
    tile = jnp.zeros((8, block.shape[1]), F32)
    for k, place in enumerate((0, 1, 6, 7)):
        row = rows_ref[k, pl.ds(level, 1), :]
        tile = jnp.where(index == place, jnp.broadcast_to(row, tile.shape), tile)
    return jnp.concatenate([block, tile], axis=0)


def laplace(value, edge_ref, sweep, level):
    size = value.shape[1]
    lane = lax.broadcasted_iota(jnp.int32, value.shape, 1)
    west = pltpu.roll(edge_ref[2 * sweep], lax.rem(size - level, size), 1)
    east = pltpu.roll(edge_ref[2 * sweep + 1], size - 1 - level, 1)
    left = jnp.where(lane == 0, west, pltpu.roll(value, 1, 1))
    right = jnp.where(lane == size - 1, east, pltpu.roll(value, size - 1, 1))
    return around(value, 0) + left + right - 4.0 * value


def sweeps(adjoint, value, spread, edge_ref, level):
    for sweep in range(SWEEPS):
        if adjoint:
            value = value + laplace(spread * value, edge_ref, sweep, level)
        else:
            value = value + spread * laplace(value, edge_ref, sweep, level)
    return value


CHUNK = 8


def gather_level(block, y_ref, x_ref, out_ref, first):
    rows_x = x_ref.shape[0]
    got = jnp.dot(
        jnp.concatenate([block, block], axis=1), y_ref[...], preferred_element_type=F32
    )
    xs = x_ref[...]
    parts = [
        jnp.sum(got[i * rows_x : (i + 1) * rows_x] * xs, axis=0, keepdims=True)
        for i in range(CHUNK)
    ]
    out_ref[pl.ds(first, CHUNK), :] = jnp.concatenate(parts, axis=0)


def gather_kernel(
    control_ref, bg_ref, rows_ref, own_ref, strips_ref, corners_ref, own_d_ref, spread_ref, req_ref,
    base_ref, delta_ref, x_ref, y_ref, d_ref, edge_ref, base_t, delta_t, inc_ref,
):
    step = pl.program_id(0)
    rows_x, rows_y = spread_ref.shape

    @pl.when(step == 0)
    def _():
        xs, ys = weight_fields(req_ref[...], rows_x, rows_y)
        x_ref[...] = xs
        high, low = split_two(ys)
        y_ref[pl.ds(0, rows_y), :] = high
        y_ref[pl.ds(rows_y, rows_y), :] = low
        d_ref[...] = extend_rows(spread_ref[...], rows_ref, rows_ref.shape[1] - 8)
        strip_setup(2, False, own_ref, strips_ref, corners_ref, (strips_ref, corners_ref, own_d_ref), edge_ref)

    spread = d_ref[...]
    for i in range(CHUNK):
        level = step * CHUNK + i
        value = extend_rows(control_ref[i], rows_ref, level)
        value = sweeps(False, value, spread, edge_ref, level)
        inc_ref[pl.ds(i * rows_x, rows_x), :] = value[:rows_x].astype(BF16)
    first = pl.multiple_of(step * CHUNK, CHUNK)
    gather_level(bg_ref[...].reshape(CHUNK * rows_x, rows_y), y_ref, x_ref, base_t, first)
    gather_level(inc_ref[...], y_ref, x_ref, delta_t, first)

    @pl.when(step == pl.num_programs(0) - 1)
    def _():
        base_ref[...] = base_t[...].T.astype(BF16)
        delta_ref[...] = delta_t[...].T.astype(BF16)


def radiance_kernel(
    cap, pos_ref, got_ref, innov_ref, var_ref, w1_ref, b1_ref, w2_ref, b2_ref, w3_ref, dep_ref, out_ref,
):
    count = pos_ref.shape[0]
    both = got_ref.shape[0]
    pos = pos_ref[...]
    peer = jnp.floor((pos.astype(F32) + 0.5) / cap).astype(jnp.int32)
    place = pos + peer * cap
    lane = lax.broadcasted_iota(jnp.int32, (count, both), 1)
    got = got_ref[...]
    pick_b = (lane == place).astype(F32).astype(BF16)
    pick_d = (lane == place + cap).astype(F32).astype(BF16)
    base = jnp.dot(pick_b, got, preferred_element_type=F32).astype(BF16)
    delta = jnp.dot(pick_d, got, preferred_element_type=F32).astype(BF16)

    def forward(a, b):
        return jnp.dot(a, b, preferred_element_type=F32)

    def backward(a, b):
        return lax.dot_general(a, b, (((1,), (1,)), ((), ())), preferred_element_type=F32)

    w1, w2, w3 = w1_ref[...], w2_ref[...], w3_ref[...]
    h_one = jnp.tanh(forward(base, w1) + b1_ref[...])
    d_one = 1.0 - h_one * h_one
    h_two = jnp.tanh(forward(h_one.astype(BF16), w2) + b2_ref[...])
    d_two = 1.0 - h_two * h_two
    t_one = (d_one * forward(delta, w1)).astype(BF16)
    t_two = (d_two * forward(t_one, w2)).astype(BF16)
    dep = (forward(t_two, w3) - innov_ref[...]) * var_ref[...]
    dep_ref[...] = dep
    s_two = (d_two * backward(dep.astype(BF16), w3)).astype(BF16)
    s_one = (d_one * backward(s_two, w2)).astype(BF16)
    grad = backward(s_one, w1).astype(BF16)
    slots = out_ref.shape[0]
    spot = lax.broadcasted_iota(jnp.int32, (count, slots), 1)
    pick = (spot == pos).astype(F32).astype(BF16)
    out_ref[...] = lax.dot_general(
        pick, grad, (((0,), (0,)), ((), ())), preferred_element_type=F32
    ).astype(BF16)


def rim_kernel(rows_x, rows_y, grad_ref, req_ref, rows_ref, strips_ref, grad_t_ref):
    xs, ys = weight_fields(req_ref[...], rows_x, rows_y)
    grad = grad_ref[...]
    grad_t = grad.astype(F32).T
    grad_t_ref[...] = grad_t
    grad_tb = grad_t.astype(BF16)
    for k, y in enumerate((0, 1, rows_y - 1, rows_y - 2)):
        high, low = split_two(xs * ys[y : y + 1])
        strips_ref[k] = jnp.dot(high, grad, preferred_element_type=F32) + jnp.dot(
            low, grad, preferred_element_type=F32
        )
    for k, x in enumerate((0, 1, rows_x - 2, rows_x - 1)):
        high, low = split_two(ys * xs[x : x + 1])
        contract = (((1,), (1,)), ((), ()))
        rows_ref[k] = lax.dot_general(
            grad_tb, high, contract, preferred_element_type=F32
        ) + lax.dot_general(grad_tb, low, contract, preferred_element_type=F32)


def adjoint_kernel(
    control_ref, grad_t_ref, req_ref, rows_ref, own_ref, strips_ref, corners_ref,
    rows_c_ref, strips_c_ref, corners_c_ref, own_d_ref, spread_ref,
    out_ref, x_ref, y_ref, d_ref, edge_ref, lhs_ref,
):
    step = pl.program_id(0)
    rows_x, rows_y = spread_ref.shape

    @pl.when(step == 0)
    def _():
        xs, ys = weight_fields(req_ref[...], rows_x, rows_y)
        x_ref[...] = xs
        high, low = split_two(ys.T)
        y_ref[:, pl.ds(0, rows_y)] = high
        y_ref[:, pl.ds(rows_y, rows_y)] = low
        d_ref[...] = extend_rows(spread_ref[...], rows_c_ref, rows_c_ref.shape[1] - 8)
        strip_setup(1, True, own_ref, strips_ref, corners_ref, (strips_c_ref, corners_c_ref, own_d_ref), edge_ref)

    xs = x_ref[...]
    for i in range(CHUNK):
        row = grad_t_ref[pl.ds(i, 1), :]
        lhs_ref[pl.ds(i * rows_x, rows_x), :] = (xs * row).astype(BF16)
    both = jnp.dot(lhs_ref[...], y_ref[...], preferred_element_type=F32)
    field = both[:, :rows_y] + both[:, rows_y:]
    spread = d_ref[...]
    for i in range(CHUNK):
        level = step * CHUNK + i
        value = extend_rows(field[i * rows_x : (i + 1) * rows_x], rows_ref, level)
        value = sweeps(True, value, spread, edge_ref, level)
        out_ref[i] = control_ref[i] + value[:rows_x]


def whole(array):
    rank = len(array.shape)
    return pl.BlockSpec(array.shape, lambda i: (0,) * rank, pipeline_mode=pl.Buffered(1))


def per_device(
    n_tile, n_obs, control, background, spread, obs_holder, obs_anchor, obs_frac, innovation,
    inverse_var, w_first, b_first, w_second, b_second, w_third,
):
    levels, rows_x, rows_y = control.shape
    owners = n_tile * n_obs
    count = obs_anchor.shape[0]
    channels = innovation.shape[1]
    cap = 3 * count // owners
    slots = owners * cap

    req, pos = pl.pallas_call(
        functools.partial(request_kernel, cap, rows_y - 1),
        out_shape=(
            jax.ShapeDtypeStruct((owners, 8, LANES), F32),
            jax.ShapeDtypeStruct((count, 1), jnp.int32),
        ),
        name="requests",
    )(obs_holder, obs_anchor.reshape(1, count), obs_frac)
    req = swap(req, n_tile, n_obs, 0)
    req = pl.pallas_call(
        functools.partial(compact_kernel, cap),
        out_shape=jax.ShapeDtypeStruct((8, slots), F32),
        name="compact",
    )(req)

    picks_x = (0, 1, rows_x - 2, rows_x - 1)
    rows = jnp.stack([control[:, x, :] for x in picks_x])
    rows_d = jnp.stack([spread[x] for x in picks_x])
    rows = jnp.concatenate([rows, jnp.broadcast_to(rows_d[:, None], (4, 8, rows_y))], axis=1)
    strips = []
    for y in (0, 1, rows_y - 1, rows_y - 2):
        strips.append(control[:, :, y].T)
        strips.append(jnp.broadcast_to(spread[:, y, None], (rows_x, levels)))
    own_c = jnp.stack([strips[0], strips[4]])
    own_d = jnp.stack([strips[1], strips[5]])
    rows_c, strips_c, corners_c = halo(rows, jnp.stack(strips), n_tile, n_obs, 2, 1)

    steps = levels // CHUNK
    block = pl.BlockSpec((CHUNK, rows_x, rows_y), lambda i: (i, 0, 0))
    column = jax.ShapeDtypeStruct((slots, levels), BF16)
    held = [rows_c, own_c, strips_c, corners_c, own_d, spread, req]
    base, delta = pl.pallas_call(
        gather_kernel,
        grid=(steps,),
        out_shape=(column, column),
        in_specs=[block, block] + [whole(a) for a in held],
        out_specs=(whole(column), whole(column)),
        scratch_shapes=[
            pltpu.VMEM((rows_x, slots), F32),
            pltpu.VMEM((2 * rows_y, slots), BF16),
            pltpu.VMEM((rows_x + 8, rows_y), F32),
            pltpu.VMEM((4, rows_x + 8, levels), F32),
            pltpu.VMEM((levels, slots), F32),
            pltpu.VMEM((levels, slots), F32),
            pltpu.VMEM((CHUNK * rows_x, rows_y), BF16),
        ],
        name="gather",
    )(control, background, *held)

    sent = jnp.concatenate(
        [base.reshape(owners, cap, levels), delta.reshape(owners, cap, levels)], axis=1
    )
    got = swap(sent, n_tile, n_obs, 2).reshape(2 * slots, levels)

    departures, grad = pl.pallas_call(
        functools.partial(radiance_kernel, cap),
        out_shape=(
            jax.ShapeDtypeStruct((count, channels), F32),
            jax.ShapeDtypeStruct((slots, levels), BF16),
        ),
        name="radiances",
    )(
        pos, got, innovation, inverse_var.reshape(1, -1), w_first, b_first.reshape(1, -1),
        w_second, b_second.reshape(1, -1), w_third,
    )
    grad = swap(grad.reshape(owners, cap, levels), n_tile, n_obs, 3).reshape(slots, levels)

    rows_a, strips_a, grad_t = pl.pallas_call(
        functools.partial(rim_kernel, rows_x, rows_y),
        out_shape=(
            jax.ShapeDtypeStruct((4, levels, rows_y), F32),
            jax.ShapeDtypeStruct((4, rows_x, levels), F32),
            jax.ShapeDtypeStruct((levels, slots), F32),
        ),
        name="rims",
    )(grad, req)
    own_a = jnp.stack([strips_a[0], strips_a[2]])
    rows_a, strips_a, corners_a = halo(rows_a, strips_a, n_tile, n_obs, 1, 4)

    held = [req, rows_a, own_a, strips_a, corners_a, rows_c, strips_c, corners_c, own_d, spread]
    gradient = pl.pallas_call(
        adjoint_kernel,
        grid=(steps,),
        out_shape=jax.ShapeDtypeStruct(control.shape, F32),
        in_specs=[block, pl.BlockSpec((CHUNK, slots), lambda i: (i, 0))] + [whole(a) for a in held],
        out_specs=block,
        scratch_shapes=[
            pltpu.VMEM((rows_x, slots), F32),
            pltpu.VMEM((slots, 2 * rows_y), BF16),
            pltpu.VMEM((rows_x + 8, rows_y), F32),
            pltpu.VMEM((4, rows_x + 8, levels), F32),
            pltpu.VMEM((CHUNK * rows_x, slots), BF16),
        ],
        name="adjoint",
    )(control, grad_t, *held)
    return (departures, gradient)


def solution(mesh):
    n_tile, n_obs = mesh.shape["tile"], mesh.shape["obs"]
    return jax.shard_map(
        functools.partial(per_device, n_tile, n_obs),
        mesh=mesh,
        in_specs=(
            P(None, "tile", "obs"),
            P(None, "tile", "obs"),
            P("tile", "obs"),
            P(("tile", "obs"), None),
            P(("tile", "obs")),
            P(None, ("tile", "obs")),
            P(("tile", "obs"), None),
            P(),
            P(),
            P(),
            P(),
            P(),
            P(),
        ),
        out_specs=(P(("tile", "obs"), None), P(None, "tile", "obs")),
        check_vma=False,
    )
```

time: 200 us -> 157 us (0.79)
  Pallas kernels: 0 us -> 115 us
  other arithmetic: 51.3 us -> 3.83 us
  waiting for transfers between devices: 39.4 us -> 0 us
  starting transfers between devices: 36.7 us -> 0 us
  local copies, waits for them, and re-layouts: 63.9 us -> 36.7 us
  matrix products: 5.8 us -> 0 us
    pallas_call x0 -> x11, Pallas kernels: none -> 115 us  [the longest x3 37.3 us: swap(): pl.pallas_call(functools.partial(swap_kernel, n_tile, n_obs), out_shape=j...]
    all_to_all x4 -> x0, waiting for transfers between devices: 32.9 us -> none  [the longest x1 20.1 us: per_device(): lax.all_to_all(pieces.reshape(owners, capacity, 4, levels).astype(jnp.bfl...]
    gather x4 -> x0, local copies, waits for them, and re-layouts: 26.2 us -> none  [the longest x1 11.5 us: per_device(): inc_cols[source].reshape(owners, capacity, 4, levels)]
    ppermute x12 -> x0, starting transfers between devices: 19.6 us -> none  [the longest x6 12.5 us: padded_2(): lax.ppermute(lax.slice_in_dim(block, 0, width, axis=dim), axis, backward)]
    scatter-add x1 -> x0, other arithmetic: 19.1 us -> none  [per_device(): gathered = jnp.zeros((rows_x * rows_y, levels), jnp.float32).at[source.re...]
    all_to_all x4 -> x0, starting transfers between devices: 17.1 us -> none  [the longest x1 5.95 us: per_device(): lax.all_to_all(inc_cols[source].reshape(owners, capacity, 4, levels), ('t...]
    slice x9 -> x5, local copies, waits for them, and re-layouts: 5.14 us -> 16.6 us  [the longest x1 13.8 us: per_device(): strips.append(control[:, :, y].T)]
    add x4 -> x0, other arithmetic: 9.77 us -> none  [the longest x1 5.22 us: advance(): crop(padded, 1)]
  transfers between devices with their start and end apart: 16 -> 0, of which waited for: 5 -> 0; matrix products, arithmetic and copies ran while one was open for 31% -> 0% of each run, Pallas kernels for 0% -> 0%
where the time goes in v1:
time: 157 us; the launch traced here: 156 us
  Pallas kernels  115 us (73%)
  local copies, waits for them, and re-layouts  36.7 us (23%)
  other arithmetic  3.83 us (2%)
    pallas_call x3, Pallas kernels, swap(): pl.pallas_call(functools.partial(swap_kernel, n_tile, n_obs), out_shape=j...  37.3 us
    pallas_call x2, Pallas kernels, halo(): pl.pallas_call(functools.partial(halo_kernel, n_tile, n_obs, k), out_shap...  28.2 us
    pallas_call x1, Pallas kernels, per_device(): pl.pallas_call(gather_kernel, grid=(steps,), out_shape=(column, column),...  20.5 us
    unnamed x29, local copies, waits for them, and re-layouts  19.3 us
    pallas_call x1, Pallas kernels, per_device(): pl.pallas_call(adjoint_kernel, grid=(steps,), out_shape=jax.ShapeDtypeStr...  17.5 us
    slice x1, local copies, waits for them, and re-layouts, per_device(): strips.append(control[:, :, y].T)  13.8 us
    pallas_call x1, Pallas kernels, per_device(): pl.pallas_call(functools.partial(radiance_kernel, cap), out_shape=(jax.Sh...  4.9 us

profile of v1, /device:TPU:0, one launch (start us, length us, event | category | flops | bytes accessed | tf_op | source)
XLA Modules:
  0.0 156.2 jit_solution(8793512772792522807)
XLA Ops:
  0.6 13.8 %fusion = (f32[128,64,1]{2,1,0:T(8,128)}, f32[128,64,1]{2,1,0:T(8,128)}, f32[128,64,1]{2,1,0:T(8,128)}, f32[128,64,1]{2,1,0:T(8,128)}) fusion(f32[128,64,128]{2,1,0:T(8,128)} %control_ref.3), kind=kLoop, calls=%fused_computation.18 | loop fusion | bytes 262144 | tf_op jit(solution)/shard_map/slice | solution.py:448
  14.4 3.8 %copy.43 = f32[128,64,1]{0,1,2:T(8,128)S(1)} copy(f32[128,64,1]{2,1,0:T(8,128)} %get-tuple-element.42) | data formatting | bytes 65536
  18.5 3.8 %copy.44 = f32[128,64,1]{0,1,2:T(8,128)S(1)} copy(f32[128,64,1]{2,1,0:T(8,128)} %get-tuple-element.41) | data formatting | bytes 65536
  22.3 3.7 %copy.45 = f32[128,64,1]{0,1,2:T(8,128)S(1)} copy(f32[128,64,1]{2,1,0:T(8,128)} %get-tuple-element.43) | data formatting | bytes 65536
  26.1 3.7 %copy.46 = f32[128,64,1]{0,1,2:T(8,128)S(1)} copy(f32[128,64,1]{2,1,0:T(8,128)} %get-tuple-element.40) | data formatting | bytes 65536
  30.0 1.8 %fusion.1 = (f32[128,1,128]{2,1,0:T(1,128)S(1)}, f32[128,1,128]{2,1,0:T(1,128)S(1)}, f32[128,1,128]{2,1,0:T(1,128)S(1)}, f32[128,1,128]{2,1,0:T(1,128)S(1)}) fusion(f32[128,64,128]{2,1,0:T(8,128)} %control_ref.3), kind=kLoop, calls=%fused_computation.19 | loop fusion | bytes 524288 | tf_op jit(solution)/shard_map/slice | solution.py:443
  31.8 0.7 pad_maximum_fusion.1.rows_ref
  32.6 15.1 %halo.2 = (f32[4,136,128]{2,1,0:T(8,128)}, f32[8,64,128]{2,1,0:T(8,128)}, f32[4,2,8,128]{3,2,1,0:T(8,128)}) custom-call(f32[4,136,128]{2,1,0:T(8,128)} %pad_maximum_fusion.1.rows_ref, f32[8,64,128]{2,1,0:T(8,128)} %copy-done.4), custom_call_target="tpu_custom_call" | custom-call | tf_op jit(solution)/shard_map/halo/pallas_call | solution.py:115
  48.5 0.8 copy.27.holder_ref
  49.3 2.4 %requests.1 = (f32[32,8,128]{2,1,0:T(8,128)}, s32[256,1]{1,0:T(8,128)}) custom-call(s32[256,1]{1,0:T(8,128)} %copy.27.holder_ref, s32[1,256]{1,0:T(1,128)} %bitcast.57, f32[2,256]{1,0:T(2,128)} %frac_ref.1), custom_call_target="tpu_custom_call" | custom-call | tf_op jit(solution)/shard_map/requests/pallas_call | solution.py:427
  51.7 9.9 %swap.3.req_ref = f32[32,8,128]{2,1,0:T(8,128)} custom-call(f32[32,8,128]{2,1,0:T(8,128)} %get-tuple-element.21.x_ref), custom_call_target="tpu_custom_call" | custom-call | tf_op jit(solution)/shard_map/swap/pallas_call | solution.py:175
  61.6 1.6 %compact.1.req_ref = f32[8,768]{1,0:T(8,128)} custom-call(f32[32,8,128]{2,1,0:T(8,128)} %swap.3.req_ref), custom_call_target="tpu_custom_call" | custom-call | tf_op jit(solution)/shard_map/compact/pallas_call | solution.py:436
  63.2 20.5 %gather.1 = (bf16[768,128]{1,0:T(8,128)(2,1)}, bf16[768,128]{1,0:T(8,128)(2,1)}) custom-call(f32[128,64,128]{2,1,0:T(8,128)} %control_ref.3, bf16[128,64,128]{2,1,0:T(8,128)(2,1)} %bg_ref.1, f32[4,136,128]{2,1,0:T(8,128)} %get-tuple-element.18.rows_ref.rows_c_ref, f32[2,64,128]{2,1,0:T(8,128)} %get-tuple-element.52.own_ref, ...), custom_call_target="tpu_custom_call" | custom-call | tf_op jit(solution)/shard_map/gather/pallas_call | solution.py:458
  83.6 1.8 %pad_maximum_fusion.x_ref = bf16[32,48,128]{2,1,0:T(8,128)(2,1)} fusion(bf16[32,24,128]{2,1,0:T(8,128)(2,1)} %bitcast.54, bf16[32,24,128]{2,1,0:T(8,128)(2,1)} %bitcast.53), kind=kLoop, calls=%fused_computation | loop fusion | flops 786432 | bytes 786432 | tf_op jit(solution)/shard_map/concatenate | solution.py:476
  85.4 14.0 %swap.4 = bf16[32,48,128]{2,1,0:T(8,128)(2,1)} custom-call(bf16[32,48,128]{2,1,0:T(8,128)(2,1)} %pad_maximum_fusion.x_ref), custom_call_target="tpu_custom_call" | custom-call | tf_op jit(solution)/shard_map/swap/pallas_call | solution.py:175
  99.5 1.1 copy.36.innov_ref
  100.6 1.1 copy.37.w3_ref
  102.2 4.9 %radiances.1 = (f32[256,616]{1,0:T(8,128)}, bf16[768,128]{1,0:T(8,128)(2,1)}) custom-call(s32[256,1]{1,0:T(8,128)} %get-tuple-element.17.pos_ref, bf16[1536,128]{1,0:T(8,128)(2,1)} %bitcast.44, f32[256,616]{1,0:T(8,128)} %copy.36.innov_ref, f32[1,616]{1,0:T(1,128)} %reshape.52.var_ref, bf16[128,512]{1,0:T(8,128)(2,1)} %w1_ref.1, f32[1,512]{1,0:T(1,128)} %bitcast.55, ...), custom_call_target="tpu_custom_call" | custom-call | tf_op jit(solution)/shard_map/radiances/pallas_call | solution.py:481
  107.1 13.4 %swap.5 = bf16[32,24,128]{2,1,0:T(8,128)(2,1)} custom-call(bf16[32,24,128]{2,1,0:T(8,128)(2,1)} %bitcast.52), custom_call_target="tpu_custom_call" | custom-call | tf_op jit(solution)/shard_map/swap/pallas_call | solution.py:175
  120.5 2.6 %rims.1 = (f32[4,128,128]{2,1,0:T(8,128)}, f32[4,64,128]{2,1,0:T(8,128)}, f32[128,768]{1,0:T(8,128)}) custom-call(bf16[768,128]{1,0:T(8,128)(2,1)} %bitcast.45, f32[8,768]{1,0:T(8,128)} %compact.1.req_ref), custom_call_target="tpu_custom_call" | custom-call | tf_op jit(solution)/shard_map/rims/pallas_call | solution.py:494
  123.1 0.8 fusion.2
  124.5 13.1 %halo.3 = (f32[4,128,128]{2,1,0:T(8,128)}, f32[4,64,128]{2,1,0:T(8,128)}, f32[4,1,8,128]{3,2,1,0:T(8,128)}) custom-call(f32[4,128,128]{2,1,0:T(8,128)} %get-tuple-element.27.rows_ref, f32[4,64,128]{2,1,0:T(8,128)} %get-tuple-element.28.strips_ref), custom_call_target="tpu_custom_call" | custom-call | tf_op jit(solution)/shard_map/halo/pallas_call | solution.py:115
  137.7 17.5 %adjoint.1 = f32[128,64,128]{2,1,0:T(8,128)} custom-call(f32[128,64,128]{2,1,0:T(8,128)} %control_ref.3, f32[128,768]{1,0:T(8,128)} %get-tuple-element.26.grad_t_ref, f32[8,768]{1,0:T(8,128)} %compact.1.req_ref, f32[4,128,128]{2,1,0:T(8,128)} %get-tuple-element.29.rows_ref, f32[2,64,128]{2,1,0:T(8,128)} %pad_maximum_fusion.4.own_ref, ...), custom_call_target="tpu_custom_call" | custom-call | tf_op jit(solution)/shard_map/adjoint/pallas_call | solution.py:507
  155.2 1.1 copy.38
  (31 shorter events, 2.6 us)
Async XLA Ops:
  14.4 3.8 %copy-start = (f32[64,128]{1,0:T(8,128)S(1)}, f32[64,128]{1,0:T(8,128)}, u32[]{:S(2)}) copy-start(f32[64,128]{1,0:T(8,128)} %spread_ref.3) | copy-start | bytes 98308
  26.0 22.4 %copy-start.6 = (s32[256,1]{0,1:T(1,128)S(1)}, s32[256,1]{0,1:T(1,128)}, u32[]{:S(2)}) copy-start(s32[256,1]{0,1:T(1,128)} %param.16) | copy-start | bytes 3076
  30.0 2.6 %copy-start.4 = (f32[8,64,128]{2,1,0:T(8,128)}, f32[8,64,128]{2,1,0:T(8,128)S(1)}, u32[]{:S(2)}) copy-start(f32[8,64,128]{2,1,0:T(8,128)S(1)} %constant_dynamic-update-slice_fusion.strips_ref) | copy-start | bytes 786436
  63.2 36.3 %copy-start.2 = (f32[256,616]{0,1:T(8,128)S(1)}, f32[256,616]{0,1:T(8,128)}, u32[]{:S(2)}) copy-start(f32[256,616]{0,1:T(8,128)} %param.19) | copy-start | bytes 1892356
  63.2 37.4 %copy-start.3 = (bf16[512,616]{0,1:T(8,128)(2,1)S(1)}, bf16[512,616]{0,1:T(8,128)(2,1)}, u32[]{:S(2)}) copy-start(bf16[512,616]{0,1:T(8,128)(2,1)} %param.25) | copy-start | bytes 1892356
  63.2 38.5 %copy-start.5 = (f32[616]{0:T(1024)S(1)}, f32[616]{0:T(1024)}, u32[]{:S(2)}) copy-start(f32[616]{0:T(1024)} %param.20) | copy-start | bytes 7396
  137.7 17.5 %copy-start.1 = (f32[256,616]{1,0:T(8,128)S(1)}, f32[256,616]{1,0:T(8,128)}, u32[]{:S(2)}) copy-start(f32[256,616]{1,0:T(8,128)} %get-tuple-element.34) | copy-start | bytes 1892356

commit v2 on v1

v2 whole, which is shorter than its diff:
```python
import functools

import jax
import jax.numpy as jnp
from jax import lax
from jax.experimental import pallas as pl
from jax.experimental.pallas import tpu as pltpu
from jax.sharding import PartitionSpec as P

SWEEPS = 2
LANES = 128
MESH_ID = pl.DeviceIdType.MESH
F32 = jnp.float32
BF16 = jnp.bfloat16


def vmem(count):
    return [pl.BlockSpec(memory_space=pltpu.VMEM)] * count


def split_two(value):
    high = value.astype(BF16)
    return high, (value - high.astype(F32)).astype(BF16)


def request_kernel(cap, per_row, holder_ref, anchor_ref, frac_ref, req_ref, pos_ref):
    owners = req_ref.shape[0]
    count = holder_ref.shape[0]
    holder = holder_ref[...]
    marks = holder == lax.broadcasted_iota(jnp.int32, (count, owners), 1)
    marks = marks.astype(F32)
    tri = lax.broadcasted_iota(jnp.int32, (count, count), 0) > lax.broadcasted_iota(
        jnp.int32, (count, count), 1
    )
    before = jnp.dot(
        tri.astype(F32).astype(BF16), marks.astype(BF16), preferred_element_type=F32
    )
    rank = jnp.sum(before * marks, axis=1, keepdims=True).astype(jnp.int32)
    pos_ref[...] = holder * cap + rank
    slot = holder * LANES + rank
    anchor = anchor_ref[...].astype(F32)
    ax = jnp.floor((anchor + 0.5) / per_row)
    ay = anchor - ax * per_row
    rows = [ax, ay]
    for axis in range(2):
        value = frac_ref[pl.ds(axis, 1), :]
        for _ in range(3):
            part = value.astype(BF16).astype(F32)
            rows.append(part)
            value = value - part
    index = lax.broadcasted_iota(jnp.int32, (8, count), 0)
    fields = jnp.zeros((8, count), F32)
    for k, row in enumerate(rows):
        fields = jnp.where(index == k, jnp.broadcast_to(row, (8, count)), fields)
    fields = fields.astype(BF16)
    step = 8
    for first in range(0, owners, step):
        lane = lax.broadcasted_iota(jnp.int32, (count, step * LANES), 1) + first * LANES
        chosen = (slot == lane).astype(F32).astype(BF16)
        got = jnp.dot(fields, chosen, preferred_element_type=F32)
        for k in range(step):
            req_ref[first + k] = got[:, k * LANES : (k + 1) * LANES]


def remote(source, target, send, recv, place):
    return pltpu.make_async_remote_copy(
        src_ref=source,
        dst_ref=target,
        send_sem=send,
        recv_sem=recv,
        device_id=place,
        device_id_type=MESH_ID,
    )


def spot(n_tile, n_obs, k):
    n = n_tile * n_obs
    me = lax.axis_index("tile") * n_obs + lax.axis_index("obs")
    peer = lax.rem(me + k, n)
    return me, peer, (peer // n_obs, lax.rem(peer, n_obs))


def greet_all(n_tile, n_obs):
    barrier = pltpu.get_barrier_semaphore()

    def greet(k, _):
        place = spot(n_tile, n_obs, k)[2]
        pl.semaphore_signal(barrier, inc=1, device_id=place, device_id_type=MESH_ID)
        return 0

    lax.fori_loop(1, n_tile * n_obs, greet, 0)


def await_all(n_tile, n_obs):
    pl.semaphore_wait(pltpu.get_barrier_semaphore(), n_tile * n_obs - 1)


def swap_start(n_tile, n_obs, x_ref, out_ref, sems):
    send_sem, recv_sem, own_sem = sems
    me = spot(n_tile, n_obs, 0)[0]

    def begin(k, _):
        _, peer, place = spot(n_tile, n_obs, k)
        remote(x_ref.at[peer], out_ref.at[me], send_sem.at[k], recv_sem.at[k], place).start()
        return 0

    lax.fori_loop(1, n_tile * n_obs, begin, 0)
    pltpu.make_async_copy(x_ref.at[me], out_ref.at[me], own_sem).start()


def swap_wait(n_tile, n_obs, x_ref, out_ref, sems):
    send_sem, recv_sem, own_sem = sems
    me = spot(n_tile, n_obs, 0)[0]

    def finish(k, _):
        _, peer, place = spot(n_tile, n_obs, k)
        remote(x_ref.at[peer], out_ref.at[me], send_sem.at[k], recv_sem.at[k], place).wait()
        return 0

    lax.fori_loop(1, n_tile * n_obs, finish, 0)
    pltpu.make_async_copy(x_ref.at[me], out_ref.at[me], own_sem).wait()


def swap_sems(n):
    return [pltpu.SemaphoreType.DMA((n,)), pltpu.SemaphoreType.DMA((n,)), pltpu.SemaphoreType.DMA]


def halo_copies(n_tile, n_obs, field, coefs, sems):
    tile, obs = lax.axis_index("tile"), lax.axis_index("obs")
    up, down = lax.rem(tile + n_tile - 1, n_tile), lax.rem(tile + 1, n_tile)
    west, east = lax.rem(obs + n_obs - 1, n_obs), lax.rem(obs + 1, n_obs)
    rows_ref, strips_ref, rows_out, strips_out, corners_out = field
    length = strips_ref.shape[1]
    top, end = pl.ds(0, 16), pl.ds(length - 16, 16)
    plan = [
        (rows_ref.at[pl.ds(0, 2)], rows_out.at[pl.ds(0, 2)], (up, obs)),
        (rows_ref.at[pl.ds(2, 2)], rows_out.at[pl.ds(2, 2)], (down, obs)),
        (strips_ref.at[pl.ds(0, 2)], strips_out.at[pl.ds(0, 2)], (tile, west)),
        (strips_ref.at[pl.ds(2, 2)], strips_out.at[pl.ds(2, 2)], (tile, east)),
        (strips_ref.at[0, top], corners_out.at[0], (up, west)),
        (strips_ref.at[0, end], corners_out.at[1], (down, west)),
        (strips_ref.at[2, top], corners_out.at[2], (up, east)),
        (strips_ref.at[2, end], corners_out.at[3], (down, east)),
    ]
    if coefs is not None:
        spread_ref, turned_ref, tiles_out = coefs
        plan += [
            (spread_ref.at[pl.ds(0, 8)], tiles_out.at[0], (up, obs)),
            (spread_ref.at[pl.ds(spread_ref.shape[0] - 8, 8)], tiles_out.at[1], (down, obs)),
            (turned_ref.at[0], tiles_out.at[2], (tile, west)),
            (turned_ref.at[1], tiles_out.at[3], (tile, east)),
            (turned_ref.at[0], tiles_out.at[4], (up, west)),
            (turned_ref.at[0], tiles_out.at[5], (down, west)),
            (turned_ref.at[1], tiles_out.at[6], (up, east)),
            (turned_ref.at[1], tiles_out.at[7], (down, east)),
        ]
    send_sem, recv_sem = sems
    return [
        remote(source, target, send_sem.at[i], recv_sem.at[i], peer)
        for i, (source, target, peer) in enumerate(plan)
    ]


def start_kernel(
    n_tile, n_obs, cap, control_ref, spread_ref, holder_ref, anchor_ref, frac_ref,
    pos_ref, req_ref, rows_out, strips_out, corners_out, own_out, tiles_out,
    ask, asked, rows_acc, strips_acc, rows_b, strips_b, turned, rows_in, strips_in, corners_in,
    tiles_in, *sems,
):
    step = pl.program_id(0)
    last = pl.num_programs(0) - 1
    _, rows_x, rows_y = control_ref.shape
    swap_set, halo_set = sems[:3], sems[3:]

    @pl.when(step == 0)
    def _():
        greet_all(n_tile, n_obs)
        request_kernel(cap, rows_y - 1, holder_ref, anchor_ref, frac_ref, ask, pos_ref)
        spread = spread_ref[...]
        square = jnp.concatenate([spread, jnp.zeros((rows_y - rows_x, rows_y), F32)], axis=0).T
        turned[0] = square[:8]
        turned[1] = square[rows_y - 8 :]
        strips_acc[...] = jnp.zeros_like(strips_acc)

    @pl.when(step == 1)
    def _():
        await_all(n_tile, n_obs)
        swap_start(n_tile, n_obs, ask, asked, swap_set)

    lane = lax.broadcasted_iota(jnp.int32, (rows_x, LANES), 1)
    first = pl.multiple_of(step * CHUNK, CHUNK)
    for k, x in enumerate((0, 1, rows_x - 2, rows_x - 1)):
        rows_acc[k, pl.ds(first, CHUNK), :] = control_ref[:, x, :]
    held = [strips_acc[k] for k in range(4)]
    for i in range(CHUNK):
        level = step * CHUNK + i
        moved = pltpu.roll(control_ref[i], level, 1)
        for k, shift in enumerate((0, 1, rows_y - 1, rows_y - 2)):
            held[k] = jnp.where(lane == lax.rem(level + shift, LANES), moved, held[k])
    for k in range(4):
        strips_acc[k] = held[k]

    @pl.when(step == last)
    def _():
        rows_b[...] = rows_acc[...].astype(BF16)
        for k, shift in enumerate((0, LANES - 1, 1, 2)):
            strip = strips_acc[k] if shift == 0 else pltpu.roll(strips_acc[k], shift, 1)
            strips_b[k] = strip.astype(BF16)
            if k % 2 == 0:
                own_out[k // 2] = strip
        copies = halo_copies(
            n_tile, n_obs, (rows_b, strips_b, rows_in, strips_in, corners_in),
            (spread_ref, turned, tiles_in), halo_set,
        )
        for copy in copies:
            copy.start()
        swap_wait(n_tile, n_obs, ask, asked, swap_set)
        req_ref[...] = jnp.concatenate(
            [asked[p][:, :cap] for p in range(n_tile * n_obs)], axis=1
        )
        for copy in copies:
            copy.wait()
        rows_out[...] = rows_in[...].astype(F32)
        strips_out[...] = strips_in[...].astype(F32)
        corners_out[...] = corners_in[...].astype(F32)
        tiles_out[...] = tiles_in[...]


def weight_fields(req, rows_x, rows_y):
    slots = req.shape[1]
    ax, ay = req[0:1].astype(jnp.int32), req[1:2].astype(jnp.int32)
    fx = req[2:3] + req[3:4] + req[4:5]
    fy = req[5:6] + req[6:7] + req[7:8]

    def ramp(size, place, frac):
        index = lax.broadcasted_iota(jnp.int32, (size, slots), 0)
        return jnp.where(index == place, 1.0 - frac, jnp.where(index == place + 1, frac, 0.0))

    return ramp(rows_x, ax, fx), ramp(rows_y, ay, fy)


def around(value, axis):
    size = value.shape[axis]
    return pltpu.roll(value, 1, axis) + pltpu.roll(value, size - 1, axis)


def strip_setup(adjoint, own_ref, strips_ref, corners_ref, tiles_ref, spread_ref, edge_ref):
    length, levels = own_ref.shape[1], own_ref.shape[2]
    index = lax.broadcasted_iota(jnp.int32, (8, levels), 0)

    def extended(base, low, high):
        return jnp.concatenate([base, jnp.where(index < 4, low, high)], axis=0)

    def plain(base):
        return jnp.concatenate([base, jnp.zeros((8, levels), F32)], axis=0)

    square = jnp.concatenate(
        [tiles_ref[t] for t in range(2, 8)] + [jnp.zeros((LANES - 48, LANES), F32)], axis=0
    ).T

    def coef(tile, row, first=0, size=length):
        at = 8 * (tile - 2) + row
        return jnp.broadcast_to(square[first : first + size, at : at + 1], (size, levels))

    size = spread_ref.shape[1]
    for side, (near, far, low, high, tile, rows, here) in enumerate(
        ((2, 3, 2, 3, 3, (7, 6), 0), (0, 1, 0, 1, 2, (0, 1), size - 1))
    ):
        s_near = extended(strips_ref[near], corners_ref[low, :8], corners_ref[high, 8:])
        s_far, s_own = plain(strips_ref[far]), plain(own_ref[side])
        d_near = extended(
            coef(tile, rows[0]),
            coef(4 + low, rows[0], 0, 8),
            coef(4 + high, rows[0], length - 8, 8),
        )
        if adjoint:
            d_far = plain(coef(tile, rows[1]))
            d_own = plain(jnp.broadcast_to(spread_ref[:, here : here + 1], (length, levels)))
            h_near = d_near * s_near
            first = s_near + around(h_near, 0) + d_far * s_far + d_own * s_own - 4.0 * h_near
            edge_ref[side] = h_near
            edge_ref[2 + side] = d_near * first
        else:
            first = s_near + d_near * (around(s_near, 0) + s_far + s_own - 4.0 * s_near)
            edge_ref[side] = s_near
            edge_ref[2 + side] = first


def extend_spread(spread_ref, tiles_ref):
    index = lax.broadcasted_iota(jnp.int32, (8, spread_ref.shape[1]), 0)
    return jnp.concatenate(
        [spread_ref[...], jnp.where(index < 4, tiles_ref[0], tiles_ref[1])], axis=0
    )


def extend_rows(block, rows_ref, level):
    index = lax.broadcasted_iota(jnp.int32, (8, block.shape[1]), 0)
    tile = jnp.zeros((8, block.shape[1]), F32)
    for k, place in enumerate((0, 1, 6, 7)):
        row = rows_ref[k, pl.ds(level, 1), :]
        tile = jnp.where(index == place, jnp.broadcast_to(row, tile.shape), tile)
    return jnp.concatenate([block, tile], axis=0)


def laplace(value, edge_ref, sweep, level):
    size = value.shape[1]
    lane = lax.broadcasted_iota(jnp.int32, value.shape, 1)
    west = pltpu.roll(edge_ref[2 * sweep], lax.rem(size - level, size), 1)
    east = pltpu.roll(edge_ref[2 * sweep + 1], size - 1 - level, 1)
    left = jnp.where(lane == 0, west, pltpu.roll(value, 1, 1))
    right = jnp.where(lane == size - 1, east, pltpu.roll(value, size - 1, 1))
    return around(value, 0) + left + right - 4.0 * value


def sweeps(adjoint, value, spread, edge_ref, level):
    for sweep in range(SWEEPS):
        if adjoint:
            value = value + laplace(spread * value, edge_ref, sweep, level)
        else:
            value = value + spread * laplace(value, edge_ref, sweep, level)
    return value


CHUNK = 8


def gather_level(block, y_ref, x_ref, out_ref, first):
    rows_x = x_ref.shape[0]
    got = jnp.dot(
        jnp.concatenate([block, block], axis=1), y_ref[...], preferred_element_type=F32
    )
    xs = x_ref[...]
    parts = [
        jnp.sum(got[i * rows_x : (i + 1) * rows_x] * xs, axis=0, keepdims=True)
        for i in range(CHUNK)
    ]
    out_ref[pl.ds(first, CHUNK), :] = jnp.concatenate(parts, axis=0)


def gather_kernel(
    n_tile, n_obs, cap, control_ref, bg_ref, rows_ref, own_ref, strips_ref, corners_ref, tiles_ref,
    spread_ref, req_ref, got_ref, x_ref, y_ref, d_ref, edge_ref, base_t, delta_t, inc_ref, sent, got,
    *sems,
):
    step = pl.program_id(0)
    rows_x, rows_y = spread_ref.shape

    @pl.when(step == 0)
    def _():
        greet_all(n_tile, n_obs)
        xs, ys = weight_fields(req_ref[...], rows_x, rows_y)
        x_ref[...] = xs
        high, low = split_two(ys)
        y_ref[pl.ds(0, rows_y), :] = high
        y_ref[pl.ds(rows_y, rows_y), :] = low
        d_ref[...] = extend_spread(spread_ref, tiles_ref)
        strip_setup(False, own_ref, strips_ref, corners_ref, tiles_ref, spread_ref, edge_ref)

    spread = d_ref[...]
    for i in range(CHUNK):
        level = step * CHUNK + i
        value = extend_rows(control_ref[i], rows_ref, level)
        value = sweeps(False, value, spread, edge_ref, level)
        inc_ref[pl.ds(i * rows_x, rows_x), :] = value[:rows_x].astype(BF16)
    first = pl.multiple_of(step * CHUNK, CHUNK)
    gather_level(bg_ref[...].reshape(CHUNK * rows_x, rows_y), y_ref, x_ref, base_t, first)
    gather_level(inc_ref[...], y_ref, x_ref, delta_t, first)

    @pl.when(step == pl.num_programs(0) - 1)
    def _():
        base, delta = base_t[...].T, delta_t[...].T
        for p in range(n_tile * n_obs):
            here = slice(p * cap, (p + 1) * cap)
            sent[p] = jnp.concatenate([base[here], delta[here]], axis=0).astype(BF16)
        await_all(n_tile, n_obs)
        swap_start(n_tile, n_obs, sent, got, sems)
        swap_wait(n_tile, n_obs, sent, got, sems)
        got_ref[...] = got[...]


def radiance_kernel(
    n_tile, n_obs, cap, rows_x, rows_y, pos_ref, got_ref, innov_ref, var_ref, w1_ref, b1_ref, w2_ref,
    b2_ref, w3_ref, req_ref, dep_ref, grad_t_ref, rows_out, strips_out, corners_out, own_out,
    sent, back, rows_b, strips_b, rows_in, strips_in, corners_in, *sems,
):
    greet_all(n_tile, n_obs)
    owners = n_tile * n_obs
    count = pos_ref.shape[0]
    both = got_ref.shape[0]
    pos = pos_ref[...]
    peer = jnp.floor((pos.astype(F32) + 0.5) / cap).astype(jnp.int32)
    place = pos + peer * cap
    lane = lax.broadcasted_iota(jnp.int32, (count, both), 1)
    got = got_ref[...]
    pick_b = (lane == place).astype(F32).astype(BF16)
    pick_d = (lane == place + cap).astype(F32).astype(BF16)
    base = jnp.dot(pick_b, got, preferred_element_type=F32).astype(BF16)
    delta = jnp.dot(pick_d, got, preferred_element_type=F32).astype(BF16)

    def forward(a, b):
        return jnp.dot(a, b, preferred_element_type=F32)

    def backward(a, b):
        return lax.dot_general(a, b, (((1,), (1,)), ((), ())), preferred_element_type=F32)

    w1, w2, w3t = w1_ref[...], w2_ref[...], w3_ref[...]
    h_one = jnp.tanh(forward(base, w1) + b1_ref[...])
    d_one = 1.0 - h_one * h_one
    h_two = jnp.tanh(forward(h_one.astype(BF16), w2) + b2_ref[...])
    d_two = 1.0 - h_two * h_two
    t_one = (d_one * forward(delta, w1)).astype(BF16)
    t_two = (d_two * forward(t_one, w2)).astype(BF16)
    dep = (backward(t_two, w3t) - innov_ref[...].T) * var_ref[...]
    dep_ref[...] = dep.T
    s_two = (d_two * forward(dep.astype(BF16), w3t)).astype(BF16)
    s_one = (d_one * backward(s_two, w2)).astype(BF16)
    grad = backward(s_one, w1).astype(BF16)
    slots = owners * cap
    spots = lax.broadcasted_iota(jnp.int32, (count, slots), 1)
    pick = (spots == pos).astype(F32).astype(BF16)
    packed = lax.dot_general(pick, grad, (((0,), (0,)), ((), ())), preferred_element_type=F32)
    for p in range(owners):
        sent[p] = packed[p * cap : (p + 1) * cap].astype(BF16)
    await_all(n_tile, n_obs)
    swap_start(n_tile, n_obs, sent, back, sems[:3])
    xs, ys = weight_fields(req_ref[...], rows_x, rows_y)
    swap_wait(n_tile, n_obs, sent, back, sems[:3])

    grad_f = jnp.concatenate([back[p].astype(F32) for p in range(owners)], axis=0)
    grad = grad_f.astype(BF16)
    grad_t = grad_f.T
    grad_t_ref[...] = grad_t
    grad_tb = grad_t.astype(BF16)
    for k, y in enumerate((0, 1, rows_y - 1, rows_y - 2)):
        high, low = split_two(xs * ys[y : y + 1])
        strip = forward(high, grad) + forward(low, grad)
        strips_b[k] = strip.astype(BF16)
        if k % 2 == 0:
            own_out[k // 2] = strip
    for k, x in enumerate((0, 1, rows_x - 2, rows_x - 1)):
        high, low = split_two(ys * xs[x : x + 1])
        rows_b[k] = (backward(grad_tb, high) + backward(grad_tb, low)).astype(BF16)
    copies = halo_copies(
        n_tile, n_obs, (rows_b, strips_b, rows_in, strips_in, corners_in), None, sems[3:]
    )
    for copy in copies:
        copy.start()
    for copy in copies:
        copy.wait()
    rows_out[...] = rows_in[...].astype(F32)
    strips_out[...] = strips_in[...].astype(F32)
    corners_out[...] = corners_in[...].astype(F32)


def adjoint_kernel(
    control_ref, grad_t_ref, req_ref, rows_ref, own_ref, strips_ref, corners_ref,
    tiles_ref, spread_ref,
    out_ref, x_ref, y_ref, d_ref, edge_ref, lhs_ref,
):
    step = pl.program_id(0)
    rows_x, rows_y = spread_ref.shape

    @pl.when(step == 0)
    def _():
        xs, ys = weight_fields(req_ref[...], rows_x, rows_y)
        x_ref[...] = xs
        high, low = split_two(ys.T)
        y_ref[:, pl.ds(0, rows_y)] = high
        y_ref[:, pl.ds(rows_y, rows_y)] = low
        d_ref[...] = extend_spread(spread_ref, tiles_ref)
        strip_setup(True, own_ref, strips_ref, corners_ref, tiles_ref, spread_ref, edge_ref)

    xs = x_ref[...]
    for i in range(CHUNK):
        row = grad_t_ref[pl.ds(i, 1), :]
        lhs_ref[pl.ds(i * rows_x, rows_x), :] = (xs * row).astype(BF16)
    both = jnp.dot(lhs_ref[...], y_ref[...], preferred_element_type=F32)
    field = both[:, :rows_y] + both[:, rows_y:]
    spread = d_ref[...]
    for i in range(CHUNK):
        level = step * CHUNK + i
        value = extend_rows(field[i * rows_x : (i + 1) * rows_x], rows_ref, level)
        value = sweeps(True, value, spread, edge_ref, level)
        out_ref[i] = control_ref[i] + value[:rows_x]


def whole(array):
    rank = len(array.shape)
    return pl.BlockSpec(array.shape, lambda i: (0,) * rank, pipeline_mode=pl.Buffered(1))


def per_device(
    n_tile, n_obs, control, background, spread, obs_holder, obs_anchor, obs_frac, innovation,
    inverse_var, w_first, b_first, w_second, b_second, w_third,
):
    levels, rows_x, rows_y = control.shape
    owners = n_tile * n_obs
    count = obs_anchor.shape[0]
    channels = innovation.shape[1]
    cap = 3 * count // owners
    slots = owners * cap

    steps = levels // CHUNK
    block = pl.BlockSpec((CHUNK, rows_x, rows_y), lambda i: (i, 0, 0))
    shape = jax.ShapeDtypeStruct
    pair, strip = shape((2, rows_x, levels), F32), shape((4, rows_x, levels), F32)
    row, corner = shape((4, levels, rows_y), F32), shape((4, 16, levels), F32)
    tiles = shape((8, 8, LANES), F32)
    landing = [
        pltpu.VMEM(row.shape, BF16),
        pltpu.VMEM(strip.shape, BF16),
        pltpu.VMEM(row.shape, BF16),
        pltpu.VMEM(strip.shape, BF16),
        pltpu.VMEM(corner.shape, BF16),
    ]
    several = pltpu.SemaphoreType.DMA

    outs = (shape((count, 1), jnp.int32), shape((8, slots), F32), row, strip, corner, pair, tiles)
    held = [spread, obs_holder, obs_anchor.reshape(1, count), obs_frac]
    pos, req, rows_c, strips_c, corners_c, own_c, tiles_c = pl.pallas_call(
        functools.partial(start_kernel, n_tile, n_obs, cap),
        grid=(steps,),
        out_shape=outs,
        in_specs=[block] + [whole(a) for a in held],
        out_specs=tuple(whole(a) for a in outs),
        scratch_shapes=[
            pltpu.VMEM((owners, 8, LANES), F32),
            pltpu.VMEM((owners, 8, LANES), F32),
            pltpu.VMEM(row.shape, F32),
            pltpu.VMEM(strip.shape, F32),
            *landing[:2],
            pltpu.VMEM((2, 8, LANES), F32),
            *landing[2:],
            pltpu.VMEM(tiles.shape, F32),
            *swap_sems(owners),
            several((16,)),
            several((16,)),
        ],
        compiler_params=pltpu.CompilerParams(collective_id=0, has_side_effects=True),
        name="start",
    )(control, *held)

    held = [rows_c, own_c, strips_c, corners_c, tiles_c, spread, req]
    column = shape((owners, 2 * cap, levels), BF16)
    got = pl.pallas_call(
        functools.partial(gather_kernel, n_tile, n_obs, cap),
        grid=(steps,),
        out_shape=column,
        in_specs=[block, block] + [whole(a) for a in held],
        out_specs=whole(column),
        scratch_shapes=[
            pltpu.VMEM((rows_x, slots), F32),
            pltpu.VMEM((2 * rows_y, slots), BF16),
            pltpu.VMEM((rows_x + 8, rows_y), F32),
            pltpu.VMEM((4, rows_x + 8, levels), F32),
            pltpu.VMEM((levels, slots), F32),
            pltpu.VMEM((levels, slots), F32),
            pltpu.VMEM((CHUNK * rows_x, rows_y), BF16),
            pltpu.VMEM(column.shape, BF16),
            pltpu.VMEM(column.shape, BF16),
            *swap_sems(owners),
        ],
        compiler_params=pltpu.CompilerParams(collective_id=1, has_side_effects=True),
        name="gather",
    )(control, background, *held)

    dep_t, grad_t, rows_a, strips_a, corners_a, own_a = pl.pallas_call(
        functools.partial(radiance_kernel, n_tile, n_obs, cap, rows_x, rows_y),
        out_shape=(
            shape((channels, count), F32), shape((levels, slots), F32), row, strip, corner, pair,
        ),
        in_specs=vmem(10),
        out_specs=tuple(vmem(6)),
        scratch_shapes=[
            pltpu.VMEM((owners, cap, levels), BF16),
            pltpu.VMEM((owners, cap, levels), BF16),
            *landing,
            *swap_sems(owners),
            several((8,)),
            several((8,)),
        ],
        compiler_params=pltpu.CompilerParams(collective_id=2, has_side_effects=True),
        name="radiances",
    )(
        pos, got.reshape(2 * slots, levels), innovation.T, inverse_var.reshape(1, -1), w_first,
        b_first.reshape(1, -1), w_second, b_second.reshape(1, -1), w_third.T, req,
    )

    held = [req, rows_a, own_a, strips_a, corners_a, tiles_c, spread]
    gradient = pl.pallas_call(
        adjoint_kernel,
        grid=(steps,),
        out_shape=jax.ShapeDtypeStruct(control.shape, F32),
        in_specs=[block, pl.BlockSpec((CHUNK, slots), lambda i: (i, 0))] + [whole(a) for a in held],
        out_specs=block,
        scratch_shapes=[
            pltpu.VMEM((rows_x, slots), F32),
            pltpu.VMEM((slots, 2 * rows_y), BF16),
            pltpu.VMEM((rows_x + 8, rows_y), F32),
            pltpu.VMEM((4, rows_x + 8, levels), F32),
            pltpu.VMEM((CHUNK * rows_x, slots), BF16),
        ],
        name="adjoint",
    )(control, grad_t, *held)
    return (dep_t.T, gradient)


def solution(mesh):
    n_tile, n_obs = mesh.shape["tile"], mesh.shape["obs"]
    return jax.shard_map(
        functools.partial(per_device, n_tile, n_obs),
        mesh=mesh,
        in_specs=(
            P(None, "tile", "obs"),
            P(None, "tile", "obs"),
            P("tile", "obs"),
            P(("tile", "obs"), None),
            P(("tile", "obs")),
            P(None, ("tile", "obs")),
            P(("tile", "obs"), None),
            P(),
            P(),
            P(),
            P(),
            P(),
            P(),
        ),
        out_specs=(P(("tile", "obs"), None), P(None, "tile", "obs")),
        check_vma=False,
    )
```

time: 157 us -> 98.2 us (0.63)
  local copies, waits for them, and re-layouts: 36.7 us -> 3.57 us
  Pallas kernels: 115 us -> 93.1 us
  other arithmetic: 3.83 us -> 0 us
    pallas_call x10 -> x3, Pallas kernels: 97.5 us -> 75.7 us  [the longest x1 29.5 us: per_device(): pl.pallas_call(functools.partial(gather_kernel, n_tile, n_obs, cap), grid...]
    unnamed x29 -> x4, local copies, waits for them, and re-layouts: 19.3 us -> 2.3 us
    slice x5 -> x0, local copies, waits for them, and re-layouts: 16.6 us -> none  [the longest x1 13.8 us: per_device(): strips.append(control[:, :, y].T)]
    concatenate x2 -> x0, other arithmetic: 2.54 us -> none  [the longest x1 1.81 us: per_device(): jnp.concatenate([base.reshape(owners, cap, levels), delta.reshape(owners,...]
where the time goes in v2:
time: 98.2 us; the launch traced here: 97.4 us
  Pallas kernels  93.1 us (95%)
  local copies, waits for them, and re-layouts  3.57 us (4%)
    pallas_call x1, Pallas kernels, per_device(): pl.pallas_call(functools.partial(gather_kernel, n_tile, n_obs, cap), grid...  29.5 us
    pallas_call x1, Pallas kernels, per_device(): pl.pallas_call(functools.partial(start_kernel, n_tile, n_obs, cap), grid=...  23.3 us
    pallas_call x1, Pallas kernels, per_device(): pl.pallas_call(functools.partial(radiance_kernel, n_tile, n_obs, cap, row...  22.9 us
    pallas_call x1, Pallas kernels, per_device(): pl.pallas_call(adjoint_kernel, grid=(steps,), out_shape=jax.ShapeDtypeStr...  17.4 us
    unnamed x4, local copies, waits for them, and re-layouts  2.3 us

profile of v2, /device:TPU:0, one launch (start us, length us, event | category | flops | bytes accessed | tf_op | source)
XLA Modules:
  0.0 97.4 jit_solution(5938291868496662385)
XLA Ops:
  0.6 1.3 %reshape.21.var_ref = f32[1,616]{1,0:T(1,128)} reshape(f32[616]{0:T(1024)} %param.20) | data formatting | bytes 4928 | tf_op jit(solution)/shard_map/reshape | solution.py:585
  1.9 1.5 %copy.15.holder_ref = s32[256,1]{1,0:T(8,128)} copy(s32[256,1]{0,1:T(1,128)} %param.16) | data formatting | bytes 2048 | tf_op args[3]
  3.4 23.3 %start.1 = (s32[256,1]{1,0:T(8,128)}, f32[8,768]{1,0:T(8,128)}, f32[4,128,128]{2,1,0:T(8,128)}, f32[4,64,128]{2,1,0:T(8,128)}, f32[4,16,128]{2,1,0:T(8,128)}, /*...) custom-call(f32[128,64,128]{2,1,0:T(8,128)} %control_ref.5, f32[64,128]{1,0:T(8,128)} %spread_ref.5, s32[256,1]{1,0:T(8,128)} %copy.15.holder_ref, ...), custom_call_target="tpu_custom_call" | custom-call | tf_op jit(solution)/shard_map/start/pallas_call | solution.py:520
  26.7 29.5 %gather.1 = bf16[32,48,128]{2,1,0:T(8,128)(2,1)} custom-call(f32[128,64,128]{2,1,0:T(8,128)} %control_ref.5, bf16[128,64,128]{2,1,0:T(8,128)(2,1)} %bg_ref.1, f32[4,128,128]{2,1,0:T(8,128)} %get-tuple-element.16.rows_ref, f32[2,64,128]{2,1,0:T(8,128)} %get-tuple-element.17.own_ref, f32[4,64,128]{2,1,0:T(8,128)} %get-tuple-element.18.strips_ref, ...), custom_call_target="tpu_custom_call" | custom-call | tf_op jit(solution)/shard_map/gather/pallas_call | solution.py:545
  56.2 22.9 %radiances.1 = (f32[616,256]{1,0:T(8,128)}, f32[128,768]{1,0:T(8,128)}, f32[4,128,128]{2,1,0:T(8,128)}, f32[4,64,128]{2,1,0:T(8,128)}, f32[4,16,128]{2,1,0:T(8,128)}, /*index=5*/f32[2,64,128]{2,1,0:T(8,128)}) custom-call(s32[256,1]{1,0:T(8,128)} %get-tuple-element.15.pos_ref, bf16[1536,128]{1,0:T(8,128)(2,1)} %bitcast.7, f32[616,256]{1,0:T(8,128)} %bitcast.8, ...), custom_call_target="tpu_custom_call" | custom-call | tf_op jit(solution)/shard_map/radiances/pallas_call | solution.py:567
  79.1 0.0 copy-start
  79.1 17.4 %adjoint.1 = f32[128,64,128]{2,1,0:T(8,128)} custom-call(f32[128,64,128]{2,1,0:T(8,128)} %control_ref.5, f32[128,768]{1,0:T(8,128)} %get-tuple-element.23.grad_t_ref, f32[8,768]{1,0:T(8,128)} %get-tuple-element.21.req_ref, f32[4,128,128]{2,1,0:T(8,128)} %get-tuple-element.24.rows_ref, f32[2,64,128]{2,1,0:T(8,128)} %get-tuple-element.25.own_ref, ...), custom_call_target="tpu_custom_call" | custom-call | tf_op jit(solution)/shard_map/adjoint/pallas_call | solution.py:590
  96.6 0.0 copy-done
  96.6 0.8 copy.17
Async XLA Ops:
  79.1 17.4 %copy-start = (f32[616,256]{1,0:T(8,128)S(1)}, f32[616,256]{1,0:T(8,128)}, u32[]{:S(2)}) copy-start(f32[616,256]{1,0:T(8,128)} %get-tuple-element.22) | copy-start | bytes 1892356

commit v3 on v2

--- a/solution.py
+++ b/solution.py
@@ -244,7 +244,7 @@
     return pltpu.roll(value, 1, axis) + pltpu.roll(value, size - 1, axis)
 
 
-def strip_setup(adjoint, own_ref, strips_ref, corners_ref, tiles_ref, spread_ref, edge_ref):
+def strip_setup(adjoint, own_ref, strips_ref, corners_ref, tiles_ref, spread_ref):
     length, levels = own_ref.shape[1], own_ref.shape[2]
     index = lax.broadcasted_iota(jnp.int32, (8, levels), 0)
 
@@ -262,9 +262,13 @@
         at = 8 * (tile - 2) + row
         return jnp.broadcast_to(square[first : first + size, at : at + 1], (size, levels))
 
+    def column(ref, at, size):
+        return jnp.broadcast_to(ref[:, at : at + 1], (size, levels))
+
     size = spread_ref.shape[1]
-    for side, (near, far, low, high, tile, rows, here) in enumerate(
-        ((2, 3, 2, 3, 3, (7, 6), 0), (0, 1, 0, 1, 2, (0, 1), size - 1))
+    parts = []
+    for side, (near, far, low, high, tile, rows, here, there) in enumerate(
+        ((2, 3, 2, 3, 3, (7, 6), 0, 1), (0, 1, 0, 1, 2, (0, 1), size - 1, size - 2))
     ):
         s_near = extended(strips_ref[near], corners_ref[low, :8], corners_ref[high, 8:])
         s_far, s_own = plain(strips_ref[far]), plain(own_ref[side])
@@ -273,52 +277,54 @@
             coef(4 + low, rows[0], 0, 8),
             coef(4 + high, rows[0], length - 8, 8),
         )
+        d_here = extended(
+            column(spread_ref, here, length),
+            column(tiles_ref.at[0], here, 8),
+            column(tiles_ref.at[1], here, 8),
+        )
         if adjoint:
             d_far = plain(coef(tile, rows[1]))
-            d_own = plain(jnp.broadcast_to(spread_ref[:, here : here + 1], (length, levels)))
-            h_near = d_near * s_near
-            first = s_near + around(h_near, 0) + d_far * s_far + d_own * s_own - 4.0 * h_near
-            edge_ref[side] = h_near
-            edge_ref[2 + side] = d_near * first
+            once = d_near * s_near
+            first = s_near + around(once, 0) + d_far * s_far + d_here * s_own - 4.0 * once
+            scaled = d_here * once
+            parts += [once + around(scaled, 0) - 4.0 * scaled + d_near * first, scaled]
         else:
             first = s_near + d_near * (around(s_near, 0) + s_far + s_own - 4.0 * s_near)
-            edge_ref[side] = s_near
-            edge_ref[2 + side] = first
-
-
-def extend_spread(spread_ref, tiles_ref):
-    index = lax.broadcasted_iota(jnp.int32, (8, spread_ref.shape[1]), 0)
-    return jnp.concatenate(
-        [spread_ref[...], jnp.where(index < 4, tiles_ref[0], tiles_ref[1])], axis=0
-    )
-
-
-def extend_rows(block, rows_ref, level):
-    index = lax.broadcasted_iota(jnp.int32, (8, block.shape[1]), 0)
-    tile = jnp.zeros((8, block.shape[1]), F32)
-    for k, place in enumerate((0, 1, 6, 7)):
-        row = rows_ref[k, pl.ds(level, 1), :]
-        tile = jnp.where(index == place, jnp.broadcast_to(row, tile.shape), tile)
-    return jnp.concatenate([block, tile], axis=0)
-
-
-def laplace(value, edge_ref, sweep, level):
-    size = value.shape[1]
-    lane = lax.broadcasted_iota(jnp.int32, value.shape, 1)
-    west = pltpu.roll(edge_ref[2 * sweep], lax.rem(size - level, size), 1)
-    east = pltpu.roll(edge_ref[2 * sweep + 1], size - 1 - level, 1)
-    left = jnp.where(lane == 0, west, pltpu.roll(value, 1, 1))
-    right = jnp.where(lane == size - 1, east, pltpu.roll(value, size - 1, 1))
-    return around(value, 0) + left + right - 4.0 * value
-
-
-def sweeps(adjoint, value, spread, edge_ref, level):
-    for sweep in range(SWEEPS):
-        if adjoint:
-            value = value + laplace(spread * value, edge_ref, sweep, level)
-        else:
-            value = value + spread * laplace(value, edge_ref, sweep, level)
-    return value
+            once = d_here * s_near
+            parts += [
+                once + d_here * (around(once, 0) - 4.0 * once + first),
+                plain(column(spread_ref, there, length)) * once,
+            ]
+    return [part[:length] for part in parts]
+
+
+PAD = 8
+
+
+def fill_spread(spread_ref, tiles_ref, d_ref):
+    rows_x = spread_ref.shape[0]
+    d_ref[pl.ds(0, PAD), :] = tiles_ref[1]
+    d_ref[pl.ds(PAD, rows_x), :] = spread_ref[...]
+    d_ref[pl.ds(PAD + rows_x, PAD), :] = tiles_ref[0]
+
+
+def rim_tiles(rows_ref, level, size):
+    index = lax.broadcasted_iota(jnp.int32, (PAD, size), 0)
+
+    def row(k):
+        return jnp.broadcast_to(rows_ref[k, pl.ds(level, 1), :], (PAD, size))
+
+    return jnp.where(index < 7, row(2), row(3)), jnp.where(index < 1, row(0), row(1))
+
+
+def laplace(buf, i, first, count):
+    centre = buf[i, pl.ds(first, count), :]
+    size = centre.shape[1]
+    lane = lax.broadcasted_iota(jnp.int32, centre.shape, 1)
+    total = buf[i, pl.ds(first - 1, count), :] + buf[i, pl.ds(first + 1, count), :]
+    total = total + jnp.where(lane == 0, 0.0, pltpu.roll(centre, 1, 1))
+    total = total + jnp.where(lane == size - 1, 0.0, pltpu.roll(centre, size - 1, 1))
+    return centre, total - 4.0 * centre
 
 
 CHUNK = 8
@@ -339,8 +345,8 @@
 
 def gather_kernel(
     n_tile, n_obs, cap, control_ref, bg_ref, rows_ref, own_ref, strips_ref, corners_ref, tiles_ref,
-    spread_ref, req_ref, got_ref, x_ref, y_ref, d_ref, edge_ref, base_t, delta_t, inc_ref, sent, got,
-    *sems,
+    spread_ref, req_ref, got_ref, x_ref, y_ref, d_ref, fix_ref, base_t, delta_t, inc_ref, buf, buf_b,
+    sent, got, *sems,
 ):
     step = pl.program_id(0)
     rows_x, rows_y = spread_ref.shape
@@ -353,22 +359,36 @@
         high, low = split_two(ys)
         y_ref[pl.ds(0, rows_y), :] = high
         y_ref[pl.ds(rows_y, rows_y), :] = low
-        d_ref[...] = extend_spread(spread_ref, tiles_ref)
-        strip_setup(False, own_ref, strips_ref, corners_ref, tiles_ref, spread_ref, edge_ref)
-
-    spread = d_ref[...]
+        fill_spread(spread_ref, tiles_ref, d_ref)
+        parts = strip_setup(False, own_ref, strips_ref, corners_ref, tiles_ref, spread_ref)
+        rims = (0, 1, rows_y - 1, rows_y - 2)
+        weights = jnp.concatenate([xs * ys[y : y + 1] for y in rims], axis=0)
+        fix_ref[...] = lax.dot_general(
+            weights.astype(BF16),
+            jnp.concatenate(parts, axis=0).astype(BF16),
+            (((0,), (0,)), ((), ())),
+            preferred_element_type=F32,
+        )
+
+    wide = rows_x + PAD
     for i in range(CHUNK):
         level = step * CHUNK + i
-        value = extend_rows(control_ref[i], rows_ref, level)
-        value = sweeps(False, value, spread, edge_ref, level)
-        inc_ref[pl.ds(i * rows_x, rows_x), :] = value[:rows_x].astype(BF16)
+        north, south = rim_tiles(rows_ref, level, rows_y)
+        buf[i, pl.ds(0, PAD), :] = north
+        buf[i, pl.ds(PAD, rows_x), :] = control_ref[i]
+        buf[i, pl.ds(PAD + rows_x, PAD), :] = south
+        centre, total = laplace(buf, i, PAD - 1, wide)
+        buf_b[i, pl.ds(PAD - 1, wide), :] = centre + d_ref[pl.ds(PAD - 1, wide), :] * total
+        centre, total = laplace(buf_b, i, PAD, rows_x)
+        value = centre + d_ref[pl.ds(PAD, rows_x), :] * total
+        inc_ref[pl.ds(i * rows_x, rows_x), :] = value.astype(BF16)
     first = pl.multiple_of(step * CHUNK, CHUNK)
     gather_level(bg_ref[...].reshape(CHUNK * rows_x, rows_y), y_ref, x_ref, base_t, first)
     gather_level(inc_ref[...], y_ref, x_ref, delta_t, first)
 
     @pl.when(step == pl.num_programs(0) - 1)
     def _():
-        base, delta = base_t[...].T, delta_t[...].T
+        base, delta = base_t[...].T, delta_t[...].T + fix_ref[...]
         for p in range(n_tile * n_obs):
             here = slice(p * cap, (p + 1) * cap)
             sent[p] = jnp.concatenate([base[here], delta[here]], axis=0).astype(BF16)
@@ -455,7 +475,7 @@
 def adjoint_kernel(
     control_ref, grad_t_ref, req_ref, rows_ref, own_ref, strips_ref, corners_ref,
     tiles_ref, spread_ref,
-    out_ref, x_ref, y_ref, d_ref, edge_ref, lhs_ref,
+    out_ref, x_ref, y_ref, d_ref, fix_ref, lhs_ref, buf, buf_b, buf_f,
 ):
     step = pl.program_id(0)
     rows_x, rows_y = spread_ref.shape
@@ -467,8 +487,15 @@
         high, low = split_two(ys.T)
         y_ref[:, pl.ds(0, rows_y)] = high
         y_ref[:, pl.ds(rows_y, rows_y)] = low
-        d_ref[...] = extend_spread(spread_ref, tiles_ref)
-        strip_setup(True, own_ref, strips_ref, corners_ref, tiles_ref, spread_ref, edge_ref)
+        fill_spread(spread_ref, tiles_ref, d_ref)
+        parts = strip_setup(True, own_ref, strips_ref, corners_ref, tiles_ref, spread_ref)
+        shifts = (0, 1, rows_y - 1, rows_y - 2)
+        moved = [p if t == 0 else pltpu.roll(p, t, 1) for p, t in zip(parts, shifts)]
+        lane = lax.broadcasted_iota(jnp.int32, (rows_x, rows_y), 1)
+        for r in range(4):
+            key = lax.rem(lane + (4 - r), 4)
+            mixed = jnp.where(key == 0, moved[0], jnp.where(key == 1, moved[1], moved[3]))
+            fix_ref[r] = jnp.where(key == 3, moved[2], mixed)
 
     xs = x_ref[...]
     for i in range(CHUNK):
@@ -476,12 +503,30 @@
         lhs_ref[pl.ds(i * rows_x, rows_x), :] = (xs * row).astype(BF16)
     both = jnp.dot(lhs_ref[...], y_ref[...], preferred_element_type=F32)
     field = both[:, :rows_y] + both[:, rows_y:]
-    spread = d_ref[...]
+    wide = rows_x + PAD
+    lane = lax.broadcasted_iota(jnp.int32, (rows_x, rows_y), 1)
+    rim = (lane < 2) | (lane >= rows_y - 2)
+    d_top, d_own, d_end = (
+        d_ref[pl.ds(0, PAD), :], d_ref[pl.ds(PAD, rows_x), :], d_ref[pl.ds(PAD + rows_x, PAD), :],
+    )
     for i in range(CHUNK):
         level = step * CHUNK + i
-        value = extend_rows(field[i * rows_x : (i + 1) * rows_x], rows_ref, level)
-        value = sweeps(True, value, spread, edge_ref, level)
-        out_ref[i] = control_ref[i] + value[:rows_x]
+        north, south = rim_tiles(rows_ref, level, rows_y)
+        own = field[i * rows_x : (i + 1) * rows_x]
+        buf_f[i, pl.ds(0, PAD), :] = north
+        buf_f[i, pl.ds(PAD, rows_x), :] = own
+        buf_f[i, pl.ds(PAD + rows_x, PAD), :] = south
+        buf[i, pl.ds(0, PAD), :] = d_top * north
+        buf[i, pl.ds(PAD, rows_x), :] = d_own * own
+        buf[i, pl.ds(PAD + rows_x, PAD), :] = d_end * south
+        total = laplace(buf, i, PAD - 1, wide)[1]
+        once = buf_f[i, pl.ds(PAD - 1, wide), :] + total
+        buf_f[i, pl.ds(PAD - 1, wide), :] = once
+        buf_b[i, pl.ds(PAD - 1, wide), :] = d_ref[pl.ds(PAD - 1, wide), :] * once
+        total = laplace(buf_b, i, PAD, rows_x)[1]
+        fix = pltpu.roll(fix_ref[i % 4], lax.rem(rows_y - level, rows_y), 1)
+        value = buf_f[i, pl.ds(PAD, rows_x), :] + total + jnp.where(rim, fix, 0.0)
+        out_ref[i] = control_ref[i] + value
 
 
 def whole(array):
@@ -514,6 +559,7 @@
         pltpu.VMEM(corner.shape, BF16),
     ]
     several = pltpu.SemaphoreType.DMA
+    padded = pltpu.VMEM((CHUNK, rows_x + 2 * PAD, rows_y), F32)
 
     outs = (shape((count, 1), jnp.int32), shape((8, slots), F32), row, strip, corner, pair, tiles)
     held = [spread, obs_holder, obs_anchor.reshape(1, count), obs_frac]
@@ -551,11 +597,13 @@
         scratch_shapes=[
             pltpu.VMEM((rows_x, slots), F32),
             pltpu.VMEM((2 * rows_y, slots), BF16),
-            pltpu.VMEM((rows_x + 8, rows_y), F32),
-            pltpu.VMEM((4, rows_x + 8, levels), F32),
+            pltpu.VMEM((rows_x + 2 * PAD, rows_y), F32),
+            pltpu.VMEM((slots, levels), F32),
             pltpu.VMEM((levels, slots), F32),
             pltpu.VMEM((levels, slots), F32),
             pltpu.VMEM((CHUNK * rows_x, rows_y), BF16),
+            padded,
+            padded,
             pltpu.VMEM(column.shape, BF16),
             pltpu.VMEM(column.shape, BF16),
             *swap_sems(owners),
@@ -596,9 +644,12 @@
         scratch_shapes=[
             pltpu.VMEM((rows_x, slots), F32),
             pltpu.VMEM((slots, 2 * rows_y), BF16),
-            pltpu.VMEM((rows_x + 8, rows_y), F32),
-            pltpu.VMEM((4, rows_x + 8, levels), F32),
+            pltpu.VMEM((rows_x + 2 * PAD, rows_y), F32),
+            pltpu.VMEM((4, rows_x, levels), F32),
             pltpu.VMEM((CHUNK * rows_x, slots), BF16),
+            padded,
+            padded,
+            padded,
         ],
         name="adjoint",
     )(control, grad_t, *held)

time: 98.2 us -> 93.4 us (0.951)
  Pallas kernels: 93.1 us -> 88.2 us
    pallas_call x1, Pallas kernels: 29.5 us -> 26.4 us  [per_device(): pl.pallas_call(functools.partial(gather_kernel, n_tile, n_obs, cap), grid...]
    pallas_call x1, Pallas kernels: 17.4 us -> 15.6 us  [per_device(): pl.pallas_call(adjoint_kernel, grid=(steps,), out_shape=jax.ShapeDtypeStr...]
where the time goes in v3:
time: 93.4 us; the launch traced here: 92.4 us
  Pallas kernels  88.2 us (94%)
  local copies, waits for them, and re-layouts  3.57 us (4%)
    pallas_call x1, Pallas kernels, per_device(): pl.pallas_call(functools.partial(gather_kernel, n_tile, n_obs, cap), grid...  26.4 us
    pallas_call x1, Pallas kernels, per_device(): pl.pallas_call(functools.partial(start_kernel, n_tile, n_obs, cap), grid=...  23.3 us
    pallas_call x1, Pallas kernels, per_device(): pl.pallas_call(functools.partial(radiance_kernel, n_tile, n_obs, cap, row...  22.9 us
    pallas_call x1, Pallas kernels, per_device(): pl.pallas_call(adjoint_kernel, grid=(steps,), out_shape=jax.ShapeDtypeStr...  15.6 us
    unnamed x4, local copies, waits for them, and re-layouts  2.3 us

profile of v3, /device:TPU:0, one launch (start us, length us, event | category | flops | bytes accessed | tf_op | source)
XLA Modules:
  0.0 92.4 jit_solution(3320119887624888777)
XLA Ops:
  0.6 1.3 %reshape.21.var_ref = f32[1,616]{1,0:T(1,128)} reshape(f32[616]{0:T(1024)} %param.20) | data formatting | bytes 4928 | tf_op jit(solution)/shard_map/reshape | solution.py:633
  1.9 1.5 %copy.15.holder_ref = s32[256,1]{1,0:T(8,128)} copy(s32[256,1]{0,1:T(1,128)} %param.16) | data formatting | bytes 2048 | tf_op args[3]
  3.4 23.3 %start.1 = (s32[256,1]{1,0:T(8,128)}, f32[8,768]{1,0:T(8,128)}, f32[4,128,128]{2,1,0:T(8,128)}, f32[4,64,128]{2,1,0:T(8,128)}, f32[4,16,128]{2,1,0:T(8,128)}, /*...) custom-call(f32[128,64,128]{2,1,0:T(8,128)} %control_ref.5, f32[64,128]{1,0:T(8,128)} %spread_ref.5, s32[256,1]{1,0:T(8,128)} %copy.15.holder_ref, ...), custom_call_target="tpu_custom_call" | custom-call | tf_op jit(solution)/shard_map/start/pallas_call | solution.py:566
  26.7 26.4 %gather.1 = bf16[32,48,128]{2,1,0:T(8,128)(2,1)} custom-call(f32[128,64,128]{2,1,0:T(8,128)} %control_ref.5, bf16[128,64,128]{2,1,0:T(8,128)(2,1)} %bg_ref.1, f32[4,128,128]{2,1,0:T(8,128)} %get-tuple-element.16.rows_ref, f32[2,64,128]{2,1,0:T(8,128)} %get-tuple-element.17.own_ref, f32[4,64,128]{2,1,0:T(8,128)} %get-tuple-element.18.strips_ref, ...), custom_call_target="tpu_custom_call" | custom-call | tf_op jit(solution)/shard_map/gather/pallas_call | solution.py:591
  53.0 22.9 %radiances.1 = (f32[616,256]{1,0:T(8,128)}, f32[128,768]{1,0:T(8,128)}, f32[4,128,128]{2,1,0:T(8,128)}, f32[4,64,128]{2,1,0:T(8,128)}, f32[4,16,128]{2,1,0:T(8,128)}, /*index=5*/f32[2,64,128]{2,1,0:T(8,128)}) custom-call(s32[256,1]{1,0:T(8,128)} %get-tuple-element.15.pos_ref, bf16[1536,128]{1,0:T(8,128)(2,1)} %bitcast.7, f32[616,256]{1,0:T(8,128)} %bitcast.8, ...), custom_call_target="tpu_custom_call" | custom-call | tf_op jit(solution)/shard_map/radiances/pallas_call | solution.py:615
  75.9 0.0 copy-start
  76.0 15.6 %adjoint.1 = f32[128,64,128]{2,1,0:T(8,128)} custom-call(f32[128,64,128]{2,1,0:T(8,128)} %control_ref.5, f32[128,768]{1,0:T(8,128)} %get-tuple-element.23.grad_t_ref, f32[8,768]{1,0:T(8,128)} %get-tuple-element.21.req_ref, f32[4,128,128]{2,1,0:T(8,128)} %get-tuple-element.24.rows_ref, f32[2,64,128]{2,1,0:T(8,128)} %get-tuple-element.25.own_ref, ...), custom_call_target="tpu_custom_call" | custom-call | tf_op jit(solution)/shard_map/adjoint/pallas_call | solution.py:638
  91.6 0.0 copy-done
  91.6 0.8 copy.17
Async XLA Ops:
  75.9 15.6 %copy-start = (f32[616,256]{1,0:T(8,128)S(1)}, f32[616,256]{1,0:T(8,128)}, u32[]{:S(2)}) copy-start(f32[616,256]{1,0:T(8,128)} %get-tuple-element.22) | copy-start | bytes 1892356

commit v4 on v3

--- a/solution.py
+++ b/solution.py
@@ -162,19 +162,21 @@
 
 
 def start_kernel(
-    n_tile, n_obs, cap, control_ref, spread_ref, holder_ref, anchor_ref, frac_ref,
-    pos_ref, req_ref, rows_out, strips_out, corners_out, own_out, tiles_out,
-    ask, asked, rows_acc, strips_acc, rows_b, strips_b, turned, rows_in, strips_in, corners_in,
+    n_tile, n_obs, cap, control_ref, bg_hbm, spread_ref, holder_ref, anchor_ref, frac_ref,
+    pos_ref, req_ref, rows_out, strips_out, corners_out, own_out, tiles_out, base_out,
+    x_ref, y_ref, bg_ref, bg_sem, ask, asked, rows_acc, strips_acc, rows_b, strips_b, turned, rows_in, strips_in, corners_in,
     tiles_in, *sems,
 ):
     step = pl.program_id(0)
-    last = pl.num_programs(0) - 1
     _, rows_x, rows_y = control_ref.shape
+    steps = base_out.shape[0] // CHUNK
+    last = steps - 1
     swap_set, halo_set = sems[:3], sems[3:]
 
     @pl.when(step == 0)
     def _():
         greet_all(n_tile, n_obs)
+        pltpu.make_async_copy(bg_hbm, bg_ref, bg_sem).start()
         request_kernel(cap, rows_y - 1, holder_ref, anchor_ref, frac_ref, ask, pos_ref)
         spread = spread_ref[...]
         square = jnp.concatenate([spread, jnp.zeros((rows_y - rows_x, rows_y), F32)], axis=0).T
@@ -182,7 +184,7 @@
         turned[1] = square[rows_y - 8 :]
         strips_acc[...] = jnp.zeros_like(strips_acc)
 
-    @pl.when(step == 1)
+    @pl.when(step == min(4, steps - 1))
     def _():
         await_all(n_tile, n_obs)
         swap_start(n_tile, n_obs, ask, asked, swap_set)
@@ -218,6 +220,16 @@
         req_ref[...] = jnp.concatenate(
             [asked[p][:, :cap] for p in range(n_tile * n_obs)], axis=1
         )
+        fill_weights(req_ref, rows_x, rows_y, x_ref, y_ref)
+        pltpu.make_async_copy(bg_hbm, bg_ref, bg_sem).wait()
+
+        def gather_base(chunk, _):
+            first = pl.multiple_of(chunk * CHUNK, CHUNK)
+            part = bg_ref[pl.ds(first, CHUNK)].reshape(CHUNK * rows_x, rows_y)
+            gather_level(part, y_ref, x_ref, base_out, first)
+            return 0
+
+        lax.fori_loop(0, steps, gather_base, 0)
         for copy in copies:
             copy.wait()
         rows_out[...] = rows_in[...].astype(F32)
@@ -343,9 +355,18 @@
     out_ref[pl.ds(first, CHUNK), :] = jnp.concatenate(parts, axis=0)
 
 
+def fill_weights(req_ref, rows_x, rows_y, x_ref, y_ref):
+    xs, ys = weight_fields(req_ref[...], rows_x, rows_y)
+    x_ref[...] = xs
+    high, low = split_two(ys)
+    y_ref[pl.ds(0, rows_y), :] = high
+    y_ref[pl.ds(rows_y, rows_y), :] = low
+    return xs, ys
+
+
 def gather_kernel(
-    n_tile, n_obs, cap, control_ref, bg_ref, rows_ref, own_ref, strips_ref, corners_ref, tiles_ref,
-    spread_ref, req_ref, got_ref, x_ref, y_ref, d_ref, fix_ref, base_t, delta_t, inc_ref, buf, buf_b,
+    n_tile, n_obs, cap, control_ref, base_ref, rows_ref, own_ref, strips_ref, corners_ref, tiles_ref,
+    spread_ref, req_ref, got_ref, x_ref, y_ref, d_ref, fix_ref, delta_t, inc_ref, buf, buf_b,
     sent, got, *sems,
 ):
     step = pl.program_id(0)
@@ -354,11 +375,7 @@
     @pl.when(step == 0)
     def _():
         greet_all(n_tile, n_obs)
-        xs, ys = weight_fields(req_ref[...], rows_x, rows_y)
-        x_ref[...] = xs
-        high, low = split_two(ys)
-        y_ref[pl.ds(0, rows_y), :] = high
-        y_ref[pl.ds(rows_y, rows_y), :] = low
+        xs, ys = fill_weights(req_ref, rows_x, rows_y, x_ref, y_ref)
         fill_spread(spread_ref, tiles_ref, d_ref)
         parts = strip_setup(False, own_ref, strips_ref, corners_ref, tiles_ref, spread_ref)
         rims = (0, 1, rows_y - 1, rows_y - 2)
@@ -383,12 +400,11 @@
         value = centre + d_ref[pl.ds(PAD, rows_x), :] * total
         inc_ref[pl.ds(i * rows_x, rows_x), :] = value.astype(BF16)
     first = pl.multiple_of(step * CHUNK, CHUNK)
-    gather_level(bg_ref[...].reshape(CHUNK * rows_x, rows_y), y_ref, x_ref, base_t, first)
     gather_level(inc_ref[...], y_ref, x_ref, delta_t, first)
 
     @pl.when(step == pl.num_programs(0) - 1)
     def _():
-        base, delta = base_t[...].T, delta_t[...].T + fix_ref[...]
+        base, delta = base_ref[...].T, delta_t[...].T + fix_ref[...]
         for p in range(n_tile * n_obs):
             here = slice(p * cap, (p + 1) * cap)
             sent[p] = jnp.concatenate([base[here], delta[here]], axis=0).astype(BF16)
@@ -562,14 +578,19 @@
     padded = pltpu.VMEM((CHUNK, rows_x + 2 * PAD, rows_y), F32)
 
     outs = (shape((count, 1), jnp.int32), shape((8, slots), F32), row, strip, corner, pair, tiles)
+    outs += (shape((levels, slots), F32),)
     held = [spread, obs_holder, obs_anchor.reshape(1, count), obs_frac]
-    pos, req, rows_c, strips_c, corners_c, own_c, tiles_c = pl.pallas_call(
+    pos, req, rows_c, strips_c, corners_c, own_c, tiles_c, base = pl.pallas_call(
         functools.partial(start_kernel, n_tile, n_obs, cap),
         grid=(steps,),
         out_shape=outs,
-        in_specs=[block] + [whole(a) for a in held],
+        in_specs=[block, pl.BlockSpec(memory_space=pl.ANY)] + [whole(a) for a in held],
         out_specs=tuple(whole(a) for a in outs),
         scratch_shapes=[
+            pltpu.VMEM((rows_x, slots), F32),
+            pltpu.VMEM((2 * rows_y, slots), BF16),
+            pltpu.VMEM(background.shape, BF16),
+            pltpu.SemaphoreType.DMA,
             pltpu.VMEM((owners, 8, LANES), F32),
             pltpu.VMEM((owners, 8, LANES), F32),
             pltpu.VMEM(row.shape, F32),
@@ -584,22 +605,21 @@
         ],
         compiler_params=pltpu.CompilerParams(collective_id=0, has_side_effects=True),
         name="start",
-    )(control, *held)
-
-    held = [rows_c, own_c, strips_c, corners_c, tiles_c, spread, req]
+    )(control, background, *held)
+
+    held = [base, rows_c, own_c, strips_c, corners_c, tiles_c, spread, req]
     column = shape((owners, 2 * cap, levels), BF16)
     got = pl.pallas_call(
         functools.partial(gather_kernel, n_tile, n_obs, cap),
         grid=(steps,),
         out_shape=column,
-        in_specs=[block, block] + [whole(a) for a in held],
+        in_specs=[block] + [whole(a) for a in held],
         out_specs=whole(column),
         scratch_shapes=[
             pltpu.VMEM((rows_x, slots), F32),
             pltpu.VMEM((2 * rows_y, slots), BF16),
             pltpu.VMEM((rows_x + 2 * PAD, rows_y), F32),
             pltpu.VMEM((slots, levels), F32),
-            pltpu.VMEM((levels, slots), F32),
             pltpu.VMEM((levels, slots), F32),
             pltpu.VMEM((CHUNK * rows_x, rows_y), BF16),
             padded,
@@ -610,7 +630,7 @@
         ],
         compiler_params=pltpu.CompilerParams(collective_id=1, has_side_effects=True),
         name="gather",
-    )(control, background, *held)
+    )(control, *held)
 
     dep_t, grad_t, rows_a, strips_a, corners_a, own_a = pl.pallas_call(
         functools.partial(radiance_kernel, n_tile, n_obs, cap, rows_x, rows_y),

time: 93.4 us -> 91.5 us (0.980)
  Pallas kernels: 88.2 us -> 86.3 us
where the time goes in v4:
time: 91.5 us; the launch traced here: 90.6 us
  Pallas kernels  86.3 us (94%)
  local copies, waits for them, and re-layouts  3.57 us (4%)
    pallas_call x1, Pallas kernels, per_device(): pl.pallas_call(functools.partial(gather_kernel, n_tile, n_obs, cap), grid...  25.7 us
    pallas_call x1, Pallas kernels, per_device(): pl.pallas_call(functools.partial(start_kernel, n_tile, n_obs, cap), grid=...  22.9 us
    pallas_call x1, Pallas kernels, per_device(): pl.pallas_call(functools.partial(radiance_kernel, n_tile, n_obs, cap, row...  22.1 us
    pallas_call x1, Pallas kernels, per_device(): pl.pallas_call(adjoint_kernel, grid=(steps,), out_shape=jax.ShapeDtypeStr...  15.6 us
    unnamed x4, local copies, waits for them, and re-layouts  2.3 us

profile of v4, /device:TPU:0, one launch (start us, length us, event | category | flops | bytes accessed | tf_op | source)
XLA Modules:
  0.0 90.6 jit_solution(16579384444307997814)
XLA Ops:
  0.6 1.3 %reshape.21.var_ref = f32[1,616]{1,0:T(1,128)} reshape(f32[616]{0:T(1024)} %param.20) | data formatting | bytes 4928 | tf_op jit(solution)/shard_map/reshape | solution.py:653
  1.9 1.5 %copy.15.holder_ref = s32[256,1]{1,0:T(8,128)} copy(s32[256,1]{0,1:T(1,128)} %param.16) | data formatting | bytes 2048 | tf_op args[3]
  3.4 22.9 %start.1 = (s32[256,1]{1,0:T(8,128)}, f32[8,768]{1,0:T(8,128)}, f32[4,128,128]{2,1,0:T(8,128)}, f32[4,64,128]{2,1,0:T(8,128)}, f32[4,16,128]{2,1,0:T(8,128)}, /*...) custom-call(f32[128,64,128]{2,1,0:T(8,128)} %control_ref.5, bf16[128,64,128]{2,1,0:T(8,128)(2,1)} %bg_hbm.1, ...), custom_call_target="tpu_custom_call" | custom-call | tf_op jit(solution)/shard_map/start/pallas_call | solution.py:583
  26.3 25.7 %gather.1 = bf16[32,48,128]{2,1,0:T(8,128)(2,1)} custom-call(f32[128,64,128]{2,1,0:T(8,128)} %control_ref.5, f32[128,768]{1,0:T(8,128)} %get-tuple-element.17.base_ref, f32[4,128,128]{2,1,0:T(8,128)} %get-tuple-element.18.rows_ref, f32[2,64,128]{2,1,0:T(8,128)} %get-tuple-element.19.own_ref, f32[4,64,128]{2,1,0:T(8,128)} %get-tuple-element.20.strips_ref, ...), custom_call_target="tpu_custom_call" | custom-call | tf_op jit(solution)/shard_map/gather/pallas_call | solution.py:612
  52.0 22.1 %radiances.1 = (f32[616,256]{1,0:T(8,128)}, f32[128,768]{1,0:T(8,128)}, f32[4,128,128]{2,1,0:T(8,128)}, f32[4,64,128]{2,1,0:T(8,128)}, f32[4,16,128]{2,1,0:T(8,128)}, /*index=5*/f32[2,64,128]{2,1,0:T(8,128)}) custom-call(s32[256,1]{1,0:T(8,128)} %get-tuple-element.16.pos_ref, bf16[1536,128]{1,0:T(8,128)(2,1)} %bitcast.7, f32[616,256]{1,0:T(8,128)} %bitcast.8, ...), custom_call_target="tpu_custom_call" | custom-call | tf_op jit(solution)/shard_map/radiances/pallas_call | solution.py:635
  74.1 0.0 copy-start
  74.1 15.6 %adjoint.1 = f32[128,64,128]{2,1,0:T(8,128)} custom-call(f32[128,64,128]{2,1,0:T(8,128)} %control_ref.5, f32[128,768]{1,0:T(8,128)} %get-tuple-element.25.grad_t_ref, f32[8,768]{1,0:T(8,128)} %get-tuple-element.23.req_ref, f32[4,128,128]{2,1,0:T(8,128)} %get-tuple-element.26.rows_ref, f32[2,64,128]{2,1,0:T(8,128)} %get-tuple-element.27.own_ref, ...), custom_call_target="tpu_custom_call" | custom-call | tf_op jit(solution)/shard_map/adjoint/pallas_call | solution.py:658
  89.7 0.0 copy-done
  89.7 0.8 copy.17
Async XLA Ops:
  74.1 15.6 %copy-start = (f32[616,256]{1,0:T(8,128)S(1)}, f32[616,256]{1,0:T(8,128)}, u32[]{:S(2)}) copy-start(f32[616,256]{1,0:T(8,128)} %get-tuple-element.24) | copy-start | bytes 1892356
